TPU v7x, 32 devices: a whole 2x2x4 slice. The times are simulated.
32 devices in a mesh: pool: 4 (over y, x), dev: 8 (over z, core).
Axes of the slice: x: 2, y: 2, z: 4, core: 2. Of those that a mesh axis runs over, the one named last changes fastest.
Arguments:
- latent: bfloat16 [4, 4, 16, 32768], P('pool', None, None, 'dev'), may hold values from -6 to 6
- tile_routes: int32 [4, 8, 4, 1], P('pool', 'dev'), may hold values from 0 to 4; in each aligned block of 4 rows (0 to 3, 4 to 7, ..., all dimensions but the last counted through in order) no two rows name the same one
- w_in: bfloat16 [4, 3, 3, 16, 128], P('pool'), may hold values from -0.5 to 0.5
- w_qkv: bfloat16 [4, 128, 384], P('pool'), may hold values from -0.5 to 0.5
- w_proj: bfloat16 [4, 128, 128], P('pool'), may hold values from -0.5 to 0.5
- w_mid: bfloat16 [4, 3, 3, 128, 128], P('pool'), may hold values from -0.1875 to 0.1875
- w_up: bfloat16 [4, 128, 512], P('pool'), may hold values from -0.5 to 0.5
- w_down: bfloat16 [4, 512, 128], P('pool'), may hold values from -0.25 to 0.25
- w_out: bfloat16 [4, 3, 3, 128, 16], P('pool'), may hold values from -0.1875 to 0.1875
- dec_in: bfloat16 [3, 3, 3, 16, 192], replicated, may hold values from -0.3125 to 0.3125
- dec_mid: bfloat16 [3, 3, 192, 192], replicated, may hold values from -0.15625 to 0.15625
Outputs:
- decoded: bfloat16 [4, 4, 192, 64, 512], P('pool', None, None, 'dev')
Inputs may be any that keep to these rules, and one draw needn't show every extreme that they name: `tile_routes`: the value 4 marks a tile without detail; a smaller value names the refiner group. Among the 4 tiles of one device no value appears more than 1 times, and in every draw some device has one value exactly 1 times.
All inputs are finite; a program needn't handle non-finite values.
Results may differ from a plain program's by a relative error of at most 0.01.
Values may be sent and summed in bfloat16 or wider, within the bound.
No kernel may reach another device: no remote copies, remote signals or barrier semaphores. Data moves between devices by JAX's collectives and lax.ppermute only.
A program may use at most 640 MiB of HBM per device.

v0:
```python
import functools
import math

import jax
import jax.numpy as jnp
from jax import lax
from jax.experimental import pallas as pl
from jax.experimental.pallas import tpu as pltpu
from jax.sharding import PartitionSpec as P

HEAD = 64
WIN = 8
LANES = 128
META = 8
EPS = 1e-06
F32 = jnp.float32
BF16 = jnp.bfloat16
VMEM_LIMIT = 60 * 2**20


def dot(a, b):
    return jnp.dot(a, b, preferred_element_type=F32)


def dot_tn(a, b):
    return lax.dot_general(a, b, (((0,), (0,)), ((), ())), preferred_element_type=F32)


def silu(x):
    half = 0.5 * x
    return half + half * jnp.tanh(half)


def norm_channels(x):
    mean = jnp.mean(x * x, axis=0, keepdims=True)
    return x * lax.rsqrt(mean + EPS)


def lane_iota(width):
    return lax.broadcasted_iota(jnp.int32, (1, width), 1)


def frame_of(group, groups, routes_ref):
    frames = groups
    named = functools.reduce(jnp.logical_or, [routes_ref[f] == group for f in range(frames)])
    wanted = jnp.where(named, group, groups)
    return sum(jnp.where(routes_ref[f] == wanted, f, 0) for f in range(frames)), named


def pick_kernel(routes_ref, tile_ref, out_ref):
    groups = pl.num_programs(0)
    group = pl.program_id(0)
    n_groups = out_ref.shape[0] * 0 + routes_ref.shape[0]
    frame, named = frame_of(group, n_groups, routes_ref)
    ch, cells = tile_ref.shape[1:]
    out_ref[0, :, :cells] = tile_ref[0]
    rows = lax.broadcasted_iota(jnp.int32, (ch, LANES), 0)
    live = jnp.where(named, 1, 0)
    out_ref[0, :, cells:] = jnp.where(rows < META, frame, live).astype(F32).astype(BF16)


def pick_tiles(routes, own_tiles, groups):
    frames, ch, cells = own_tiles.shape
    assert frames == groups
    return pl.pallas_call(
        pick_kernel,
        out_shape=jax.ShapeDtypeStruct((groups, ch, cells + LANES), BF16),
        grid_spec=pltpu.PrefetchScalarGridSpec(
            num_scalar_prefetch=1,
            grid=(groups,),
            in_specs=[
                pl.BlockSpec(
                    (1, ch, cells), lambda g, r: (frame_of(g, groups, r)[0], 0, 0)
                )
            ],
            out_specs=pl.BlockSpec((1, ch, cells + LANES), lambda g, r: (g, 0, 0)),
        ),
        name="pick",
    )(routes, own_tiles)


def refine_kernel(
    tile_ref, w_in, w_qkv, w_proj, w_mid, w_up, w_down, w_out, out_ref,
    t_in, t_qkv, t_proj, t_mid, t_up, t_down, perm, patch, att, even, odd, taps, padded,
    *, side, bands,
):
    ch = tile_ref.shape[1]
    cells = side * side
    hid = w_proj.shape[0]
    chunk = WIN * side
    chunks = cells // chunk
    heads = hid // HEAD
    win_cells = WIN * WIN
    pair = LANES // win_cells
    assert side == WIN * WIN and pair == 2 and 2 * side == LANES

    @pl.when(pl.program_id(0) == 0)
    def _():
        t_in[...] = w_in[...].astype(F32).T.astype(BF16)
        t_qkv[...] = w_qkv[...].astype(F32).T.astype(BF16)
        t_proj[...] = w_proj[...].astype(F32).T.astype(BF16)
        t_mid[...] = w_mid[...].astype(F32).T.astype(BF16)
        t_up[...] = w_up[...].astype(F32).T.astype(BF16)
        t_down[...] = w_down[...].astype(F32).T.astype(BF16)
        src = lax.broadcasted_iota(jnp.int32, (chunk, chunk), 0)
        dst = lax.broadcasted_iota(jnp.int32, (chunk, chunk), 1)
        want = ((dst >> 3) & 7) * side + (dst >> 6) * WIN + (dst & 7)
        perm[...] = jnp.where(src == want, 1.0, 0.0).astype(BF16)
        even[:, :LANES] = jnp.zeros((3 * hid, LANES), BF16)
        even[:, LANES + cells :] = jnp.zeros((3 * hid, LANES), BF16)
        padded[:, :LANES] = jnp.zeros((ch, LANES), BF16)
        padded[:, LANES + cells :] = jnp.zeros((ch, LANES), BF16)

    tile = tile_ref[0, :, :cells].astype(F32)
    lane = lane_iota(cells)
    row = lane >> 6
    col = lane & (side - 1)

    def inside(dy, dx):
        ok = None
        for pos, off in ((row, dy), (col, dx)):
            if off:
                good = (pos > 0) if off < 0 else (pos < side - 1)
                ok = good if ok is None else ok & good
        return ok

    def moved(x, dy, dx):
        off = dy * side + dx
        if off == 0:
            return x
        x = pltpu.roll(x, (-off) % cells, 1)
        return jnp.where(inside(dy, dx), x, 0.0)

    offsets = [(dy, dx) for dy in (-1, 0, 1) for dx in (-1, 0, 1)]
    for t, (dy, dx) in enumerate(offsets):
        patch[t * ch : (t + 1) * ch, :] = moved(tile, dy, dx).astype(BF16)

    low = lane_iota(LANES) < win_cells
    ccol = lane_iota(chunk) & (side - 1)
    scale = math.log2(math.e) / math.sqrt(HEAD)

    def attend(c, _):
        base = pl.multiple_of(c * chunk, chunk)
        lifted = dot(t_in[...], patch[:, pl.ds(base, chunk)])
        normed = norm_channels(lifted).astype(BF16)
        windows = dot(normed, perm[...]).astype(BF16)
        qkv = dot(t_qkv[...], windows).astype(BF16)
        mixed = []
        for h in range(heads):
            parts = []
            for p in range(chunk // LANES):
                def piece(kind):
                    top = kind * hid + h * HEAD
                    return qkv[top : top + HEAD, p * LANES : (p + 1) * LANES]
                scores = dot_tn(piece(1), piece(0))
                scores = jnp.where(low, scores[:win_cells], scores[win_cells:])
                top = jnp.max(scores, axis=0, keepdims=True)
                raised = jnp.exp2((scores - top) * scale)
                total = jnp.sum(raised, axis=0, keepdims=True)
                probs = raised * (1.0 / total)
                spread = jnp.concatenate(
                    [jnp.where(low, probs, 0.0), jnp.where(low, 0.0, probs)], axis=0
                ).astype(BF16)
                parts.append(dot(piece(2), spread))
            mixed.append(jnp.concatenate(parts, axis=1))
        mixed = jnp.concatenate(mixed, axis=0).astype(BF16)
        mixed = dot(mixed, perm[...]).astype(BF16)
        attended = lifted + dot(t_proj[...], mixed)
        att[:, pl.ds(base, chunk)] = attended
        conv_in = norm_channels(attended)
        left = jnp.where(ccol > 0, pltpu.roll(conv_in, 1, 1), 0.0)
        right = jnp.where(ccol < side - 1, pltpu.roll(conv_in, chunk - 1, 1), 0.0)
        here = pl.ds(pl.multiple_of(base + LANES, LANES), chunk)
        even[:hid, here] = left.astype(BF16)
        even[hid : 2 * hid, here] = conv_in.astype(BF16)
        even[2 * hid :, here] = right.astype(BF16)
        around = even[:, pl.ds(base, chunk + LANES)]
        odd[:, pl.ds(base, chunk)] = around[:, side : side + chunk]
        return 0

    lax.fori_loop(0, chunks, attend, 0)
    odd[:, cells:] = even[:, cells : cells + 2 * LANES][:, side : side + LANES]

    def finish(c, _):
        base = pl.multiple_of(c * chunk, chunk)
        after = pl.ds(pl.multiple_of(base + LANES, LANES), chunk)
        around = jnp.concatenate(
            [odd[:, pl.ds(base, chunk)], even[:, after], odd[:, after]], axis=0
        )
        convolved = att[:, pl.ds(base, chunk)] + silu(dot(t_mid[...], around))
        mlp_in = norm_channels(convolved).astype(BF16)
        expanded = silu(dot(t_up[...], mlp_in)).astype(BF16)
        finished = convolved + dot(t_down[...], expanded)
        taps[:, pl.ds(base, chunk)] = dot(w_out[...], finished.astype(BF16))
        return 0

    lax.fori_loop(0, chunks, finish, 0)

    delta = jnp.zeros((ch, cells), F32)
    for t, (dy, dx) in enumerate(offsets):
        delta = delta + moved(taps[t * ch : (t + 1) * ch, :], dy, dx)
    delta = delta.astype(BF16).astype(F32)
    note = tile_ref[0, :, cells:]
    live = note[META : META + 1, :1].astype(F32)
    padded[:, LANES : LANES + cells] = (tile + live * delta).astype(BF16)
    band = cells // bands
    pieces = (band + 2 * LANES) // LANES
    for b in range(bands):
        for j in range(pieces):
            at = b * band + j * LANES
            out_ref[b, j * ch : (j + 1) * ch, :] = padded[:, at : at + LANES]
        out_ref[b, pieces * ch :, :] = note[:META, :]


def refine_tiles(tiles, weights, bands):
    count, ch, width = tiles.shape
    cells = width - LANES
    side = math.isqrt(cells)
    w_in, w_qkv, w_proj, w_mid, w_up, w_down, w_out = weights
    hid = w_proj.shape[0]
    mlp = w_up.shape[1]
    w_in = w_in.reshape(-1, hid)
    w_mid = w_mid.reshape(-1, hid)
    w_out = jnp.swapaxes(w_out, 2, 3).reshape(-1, hid)
    taps = w_out.shape[0]
    chunk = WIN * side
    rows = (cells // bands + 2 * LANES) // LANES * ch + META
    whole = pl.BlockSpec(memory_space=pltpu.VMEM)
    return pl.pallas_call(
        functools.partial(refine_kernel, side=side, bands=bands),
        out_shape=jax.ShapeDtypeStruct((count * bands, rows, LANES), BF16),
        grid=(count,),
        in_specs=[pl.BlockSpec((1, ch, width), lambda i: (i, 0, 0))] + [whole] * 7,
        out_specs=pl.BlockSpec((bands, rows, LANES), lambda i: (i, 0, 0)),
        scratch_shapes=[
            pltpu.VMEM((hid, w_in.shape[0]), BF16),
            pltpu.VMEM((3 * hid, hid), BF16),
            pltpu.VMEM((hid, hid), BF16),
            pltpu.VMEM((hid, w_mid.shape[0]), BF16),
            pltpu.VMEM((mlp, hid), BF16),
            pltpu.VMEM((hid, mlp), BF16),
            pltpu.VMEM((chunk, chunk), BF16),
            pltpu.VMEM((w_in.shape[0], cells), BF16),
            pltpu.VMEM((hid, cells), F32),
            pltpu.VMEM((3 * hid, cells + 2 * LANES), BF16),
            pltpu.VMEM((3 * hid, cells + LANES), BF16),
            pltpu.VMEM((taps, cells), F32),
            pltpu.VMEM((ch, cells + 2 * LANES), BF16),
        ],
        compiler_params=pltpu.CompilerParams(vmem_limit_bytes=VMEM_LIMIT),
        name="refine",
    )(tiles, w_in, w_qkv, w_proj, w_mid, w_up, w_down, w_out)


def decode_kernel(
    where_ref, pieces_ref, w_in, w_mid, out_ref, t_in, t_mid, strip, act, rows_out,
    *, groups, lanes_in_strip, side,
):
    frames, _, ch3, cols = strip.shape
    frames -= 2
    ch = pieces_ref.shape[1] * 0 + ch3
    frame = pl.program_id(0)
    band = out_ref.shape[2]
    dec = out_ref.shape[1]
    tall = band + 4
    ch = w_in.shape[0] // 27
    columns = lanes_in_strip
    lane = lane_iota(LANES)
    low = lane < side
    col = lane_iota(cols)

    @pl.when(frame == 0)
    def _():
        t_in[...] = w_in[...].astype(F32).T.astype(BF16)
        t_mid[...] = w_mid[...].astype(F32).T.astype(BF16)
        strip[0:2] = jnp.zeros((2,) + strip.shape[1:], BF16)
        note_at = tall * side // LANES * ch
        notes = [
            [pieces_ref[g * columns + d, note_at : note_at + 1, :].astype(F32) for d in range(columns)]
            for g in range(groups)
        ]
        for f in range(frames):
            picks = [
                [jnp.where(notes[g][d] == f, 1.0, 0.0) for d in range(columns)]
                for g in range(groups)
            ]
            for j in range(tall // 2):
                both = []
                for d in range(columns):
                    both.append(
                        sum(
                            pieces_ref[g * columns + d, j * ch : (j + 1) * ch, :].astype(F32)
                            * picks[g][d]
                            for g in range(groups)
                        )
                    )
                turned = [pltpu.roll(x, side, 1) for x in both]
                first = [
                    jnp.where(low, both[d], turned[d + 1]) for d in range(0, columns, 2)
                ]
                second = [
                    jnp.where(low, turned[d], both[d + 1]) for d in range(0, columns, 2)
                ]
                for y, parts in ((2 * j, first), (2 * j + 1, second)):
                    line = jnp.concatenate(parts, axis=1)
                    left = jnp.where(col > 0, pltpu.roll(line, 1, 1), 0.0)
                    right = jnp.where(col < cols - 1, pltpu.roll(line, cols - 1, 1), 0.0)
                    strip[f + 2, y] = jnp.concatenate([left, line, right], axis=0).astype(BF16)

    first_row = where_ref[0] == 0
    last_row = where_ref[0] == where_ref[1] - 1

    def act_row(y, _):
        around = jnp.concatenate(
            [
                strip[pl.ds(frame + dt, 1), pl.ds(y + dy, 1)].reshape(3 * ch, cols)
                for dt in range(3)
                for dy in range(3)
            ],
            axis=0,
        )
        value = silu(dot(t_in[...], around))
        outside = (first_row & (y == 0)) | (last_row & (y == band + 1))
        value = jnp.where(outside, 0.0, value)
        left = jnp.where(col > 0, pltpu.roll(value, 1, 1), 0.0)
        right = jnp.where(col < cols - 1, pltpu.roll(value, cols - 1, 1), 0.0)
        base = pl.multiple_of(y * 3 * dec, 3 * dec)
        act[pl.ds(base, dec), :] = left.astype(BF16)
        act[pl.ds(base + dec, dec), :] = value.astype(BF16)
        act[pl.ds(base + 2 * dec, dec), :] = right.astype(BF16)
        return 0

    lax.fori_loop(0, band + 2, act_row, 0)

    def out_row(y, _):
        base = pl.multiple_of(y * 3 * dec, 3 * dec)
        value = dot(t_mid[...], act[pl.ds(base, 9 * dec), :])
        value = value + act[pl.ds(base + 4 * dec, dec), :].astype(F32)
        for k in range(cols // LANES):
            rows_out[pl.ds(k * dec * band + y, dec, stride=band), :] = value[
                :, k * LANES : (k + 1) * LANES
            ]
        return 0

    lax.fori_loop(0, band, out_row, 0)
    for k in range(cols // LANES):
        done = rows_out[k * dec * band : (k + 1) * dec * band, :]
        out_ref[0, :, :, k * LANES : (k + 1) * LANES] = done.reshape(dec, band, LANES).astype(BF16)


def decode_band(where, pieces, dec_in, dec_mid, frames, groups, columns, side):
    ch, dec = dec_in.shape[3:]
    count, rows, _ = pieces.shape
    band = (rows - META) // ch * LANES // side - 4
    cols = columns * side
    whole = pl.BlockSpec(memory_space=pltpu.VMEM)
    w_in = dec_in.reshape(-1, dec)
    w_mid = dec_mid.reshape(-1, dec)
    return pl.pallas_call(
        functools.partial(decode_kernel, groups=groups, lanes_in_strip=columns, side=side),
        out_shape=jax.ShapeDtypeStruct((frames, dec, band, cols), BF16),
        grid_spec=pltpu.PrefetchScalarGridSpec(
            num_scalar_prefetch=1,
            grid=(frames,),
            in_specs=[whole, whole, whole],
            out_specs=pl.BlockSpec((1, dec, band, cols), lambda f, w: (f, 0, 0, 0)),
            scratch_shapes=[
                pltpu.VMEM((dec, w_in.shape[0]), BF16),
                pltpu.VMEM((dec, w_mid.shape[0]), BF16),
                pltpu.VMEM((frames + 2, band + 4, 3 * ch, cols), BF16),
                pltpu.VMEM(((band + 2) * 3 * dec, cols), BF16),
                pltpu.VMEM((cols // LANES * dec * band, LANES), F32),
            ],
        ),
        compiler_params=pltpu.CompilerParams(vmem_limit_bytes=VMEM_LIMIT),
        name="decode",
    )(where, pieces, w_in, w_mid)


def shards(latent, tile_routes, w_in, w_qkv, w_proj, w_mid, w_up, w_down, w_out, dec_in, dec_mid):
    groups = lax.axis_size("pool")
    columns = lax.axis_size("dev")
    own_tiles = latent[0]
    frames, ch, cells = own_tiles.shape
    side = math.isqrt(cells)
    outgoing = pick_tiles(tile_routes.reshape(-1), own_tiles, groups)
    landing = lax.all_to_all(outgoing, "pool", split_axis=0, concat_axis=0, tiled=True)
    weights = (w_in[0], w_qkv[0], w_proj[0], w_mid[0], w_up[0], w_down[0], w_out[0])
    chunks = refine_tiles(landing, weights, columns)
    pieces = lax.all_to_all(chunks, ("pool", "dev"), split_axis=0, concat_axis=0, tiled=True)
    where = jnp.stack([lax.axis_index("dev"), jnp.int32(columns)])
    return decode_band(where, pieces, dec_in, dec_mid, frames, groups, columns, side)[None]


def solution(mesh):
    in_specs = (
        P("pool", None, None, "dev"),
        P("pool", "dev", None, None),
        P("pool", None, None, None, None),
        P("pool", None, None),
        P("pool", None, None),
        P("pool", None, None, None, None),
        P("pool", None, None),
        P("pool", None, None),
        P("pool", None, None, None, None),
        P(),
        P(),
    )
    out_specs = P("pool", None, None, "dev", None)
    return jax.shard_map(shards, mesh=mesh, in_specs=in_specs, out_specs=out_specs, check_vma=False)
```

profile of v0, /device:TPU:0, one launch (start us, length us, event | category | flops | bytes accessed | tf_op | source)
XLA Modules:
  0.0 231.3 jit_solution(15631935933535467167)
XLA Ops:
  0.0 3.8 %pick.1 = bf16[4,16,4224]{2,1,0:T(8,128)(2,1)} custom-call(s32[4]{0:T(128)} %bitcast.27, bf16[4,16,4096]{2,1,0:T(8,128)(2,1)} %bitcast.18), custom_call_target="tpu_custom_call" | custom-call | tf_op jit(solution)/shard_map/pick/pallas_call | solution.py:65
  3.8 14.8 %all_to_all.10.tile_ref = bf16[4,16,4224]{2,1,0:T(8,128)(2,1)} all-to-all(bf16[4,16,4224]{2,1,0:T(8,128)(2,1)} %pick.1), channel_id=1, replica_groups=mesh['pool'=4,'dev'=8] {'pool'}, dimensions={0} | all-to-all | bytes 1081344 | tf_op jit(solution)/shard_map/all_to_all | solution.py:387
  18.6 140.2 %refine.1 = bf16[32,104,128]{2,1,0:T(8,128)(2,1)} custom-call(bf16[4,16,4224]{2,1,0:T(8,128)(2,1)} %all_to_all.10.tile_ref, bf16[144,128]{1,0:T(8,128)(2,1)} %bitcast.24, bf16[128,384]{1,0:T(8,128)(2,1)} %bitcast.23, bf16[128,128]{1,0:T(8,128)(2,1)} %bitcast.26, bf16[1152,128]{1,0:T(8,128)(2,1)} %bitcast.19, bf16[128,512]{1,0:T(8,128)(2,1)} %bitcast.21, ...), custom_call_target="tpu_custom_call" | custom-call | tf_op jit(solution)/shard_map/refine/pallas_call | solution.py:229
  158.8 4.2 %all-to-all-start.1 = ((bf16[32,104,128]{2,1,0:T(8,128)(2,1)}), bf16[32,104,128]{2,1,0:T(8,128)(2,1)S(1)}, u32[]{:S(2)}, u32[]{:S(2)}) async-start(bf16[32,104,128]{2,1,0:T(8,128)(2,1)} %refine.1), calls=%async_computation.1 | async-start | bytes 1703936 | tf_op jit(solution)/shard_map/all_to_all | solution.py:390
  163.1 0.7 pad_add_fusion.where_ref
  163.7 22.6 %all-to-all-done.1.pieces_ref = bf16[32,104,128]{2,1,0:T(8,128)(2,1)S(1)} async-done(((bf16[32,104,128]{2,1,0:T(8,128)(2,1)}), bf16[32,104,128]{2,1,0:T(8,128)(2,1)S(1)}, u32[]{:S(2)}, u32[]{:S(2)}) %all-to-all-start.1) | async-done | bytes 852000 | tf_op jit(solution)/shard_map/all_to_all | solution.py:390
  186.3 0.0 copy-start
  186.3 0.9 copy-done
  187.2 44.1 %decode.1 = bf16[4,192,8,512]{3,2,1,0:T(8,128)(2,1)} custom-call(s32[2]{0:T(128)} %pad_add_fusion.where_ref, bf16[32,104,128]{2,1,0:T(8,128)(2,1)} %copy-done, bf16[432,192]{1,0:T(8,128)(2,1)} %bitcast.20, bf16[1728,192]{1,0:T(8,128)(2,1)} %bitcast.17), custom_call_target="tpu_custom_call" | custom-call | tf_op jit(solution)/shard_map/decode/pallas_call | solution.py:359
Async XLA Ops:
  158.8 27.5 %all-to-all-start.1 = ((bf16[32,104,128]{2,1,0:T(8,128)(2,1)}), bf16[32,104,128]{2,1,0:T(8,128)(2,1)S(1)}, u32[]{:S(2)}, u32[]{:S(2)}) async-start(bf16[32,104,128]{2,1,0:T(8,128)(2,1)} %refine.1), calls=%async_computation.1 | async-start | bytes 1703936 | tf_op jit(solution)/shard_map/all_to_all | solution.py:390
  186.3 0.9 copy-start
where the time goes:
time: 232 us; the launch traced here: 231 us
  Pallas kernels  188 us (81%)
  waiting for transfers between devices  22.6 us (10%)
  blocking collectives  14.8 us (6%)
  starting transfers between devices  4.2 us (2%)
    pallas_call x1, Pallas kernels, refine_tiles(): pl.pallas_call(functools.partial(refine_kernel, side=side, bands=bands),...  140 us
    pallas_call x1, Pallas kernels, decode_band(): pl.pallas_call(functools.partial(decode_kernel, groups=groups, lanes_in_s...  44.1 us
    all_to_all x1, waiting for transfers between devices, shards(): lax.all_to_all(chunks, ('pool', 'dev'), split_axis=0, concat_axis=0, tile...  22.6 us
    all_to_all x1, blocking collectives, shards(): lax.all_to_all(outgoing, 'pool', split_axis=0, concat_axis=0, tiled=True)  14.8 us
  transfers between devices with their start and end apart: 1, of which 1 were waited for; matrix products, arithmetic and copies ran while one was open for 0% of the time, Pallas kernels for 0%

commit v1 on v0

--- a/solution.py
+++ b/solution.py
@@ -40,53 +40,47 @@
     return lax.broadcasted_iota(jnp.int32, (1, width), 1)
 
 
-def frame_of(group, groups, routes_ref):
-    frames = groups
-    named = functools.reduce(jnp.logical_or, [routes_ref[f] == group for f in range(frames)])
-    wanted = jnp.where(named, group, groups)
-    return sum(jnp.where(routes_ref[f] == wanted, f, 0) for f in range(frames)), named
-
-
 def pick_kernel(routes_ref, tile_ref, out_ref):
-    groups = pl.num_programs(0)
-    group = pl.program_id(0)
-    n_groups = out_ref.shape[0] * 0 + routes_ref.shape[0]
-    frame, named = frame_of(group, n_groups, routes_ref)
-    ch, cells = tile_ref.shape[1:]
-    out_ref[0, :, :cells] = tile_ref[0]
+    groups, ch, width = out_ref.shape
+    frames, _, cells = tile_ref.shape
     rows = lax.broadcasted_iota(jnp.int32, (ch, LANES), 0)
-    live = jnp.where(named, 1, 0)
-    out_ref[0, :, cells:] = jnp.where(rows < META, frame, live).astype(F32).astype(BF16)
+    for group in range(groups):
+        named = functools.reduce(
+            jnp.logical_or, [routes_ref[f] == group for f in range(frames)]
+        )
+        wanted = jnp.where(named, group, groups)
+        frame = sum(jnp.where(routes_ref[f] == wanted, f, 0) for f in range(frames))
+        out_ref[group, :, :cells] = tile_ref[frame]
+        live = jnp.where(named, 1, 0)
+        out_ref[group, :, cells:] = jnp.where(rows < META, frame, live).astype(F32).astype(BF16)
 
 
 def pick_tiles(routes, own_tiles, groups):
     frames, ch, cells = own_tiles.shape
     assert frames == groups
+    whole = pl.BlockSpec(memory_space=pltpu.VMEM)
     return pl.pallas_call(
         pick_kernel,
         out_shape=jax.ShapeDtypeStruct((groups, ch, cells + LANES), BF16),
-        grid_spec=pltpu.PrefetchScalarGridSpec(
-            num_scalar_prefetch=1,
-            grid=(groups,),
-            in_specs=[
-                pl.BlockSpec(
-                    (1, ch, cells), lambda g, r: (frame_of(g, groups, r)[0], 0, 0)
-                )
-            ],
-            out_specs=pl.BlockSpec((1, ch, cells + LANES), lambda g, r: (g, 0, 0)),
-        ),
+        in_specs=[pl.BlockSpec(memory_space=pltpu.SMEM), whole],
+        out_specs=whole,
         name="pick",
     )(routes, own_tiles)
 
 
-def refine_kernel(
-    tile_ref, w_in, w_qkv, w_proj, w_mid, w_up, w_down, w_out, out_ref,
-    t_in, t_qkv, t_proj, t_mid, t_up, t_down, perm, patch, att, even, odd, taps, padded,
-    *, side, bands,
-):
+def refine_kernel(*refs, side, bands, first):
+    if first:
+        _, tile_ref, w_in, w_qkv, w_proj, w_mid, w_up, w_down, w_out = refs[:9]
+        out_ref, t_in, t_qkv, t_proj, t_mid, t_up, t_down, perm = refs[9:17]
+        scratch = refs[17:]
+    else:
+        _, tile_ref, _, w_out, t_in, t_qkv, t_proj, t_mid, t_up, t_down, perm = refs[:11]
+        out_ref = refs[11]
+        scratch = refs[12:]
+    patch, att, even, odd, taps, padded, qkv_ref, mixed_ref = scratch
     ch = tile_ref.shape[1]
     cells = side * side
-    hid = w_proj.shape[0]
+    hid = t_proj.shape[0]
     chunk = WIN * side
     chunks = cells // chunk
     heads = hid // HEAD
@@ -94,18 +88,19 @@
     pair = LANES // win_cells
     assert side == WIN * WIN and pair == 2 and 2 * side == LANES
 
-    @pl.when(pl.program_id(0) == 0)
-    def _():
-        t_in[...] = w_in[...].astype(F32).T.astype(BF16)
-        t_qkv[...] = w_qkv[...].astype(F32).T.astype(BF16)
-        t_proj[...] = w_proj[...].astype(F32).T.astype(BF16)
-        t_mid[...] = w_mid[...].astype(F32).T.astype(BF16)
-        t_up[...] = w_up[...].astype(F32).T.astype(BF16)
-        t_down[...] = w_down[...].astype(F32).T.astype(BF16)
+    if first:
+        for flipped, weight in (
+            (t_in, w_in), (t_qkv, w_qkv), (t_proj, w_proj),
+            (t_mid, w_mid), (t_up, w_up), (t_down, w_down),
+        ):
+            flipped[...] = weight[...].astype(F32).T.astype(BF16)
         src = lax.broadcasted_iota(jnp.int32, (chunk, chunk), 0)
         dst = lax.broadcasted_iota(jnp.int32, (chunk, chunk), 1)
         want = ((dst >> 3) & 7) * side + (dst >> 6) * WIN + (dst & 7)
         perm[...] = jnp.where(src == want, 1.0, 0.0).astype(BF16)
+
+    @pl.when(pl.program_id(0) == 0)
+    def _():
         even[:, :LANES] = jnp.zeros((3 * hid, LANES), BF16)
         even[:, LANES + cells :] = jnp.zeros((3 * hid, LANES), BF16)
         padded[:, :LANES] = jnp.zeros((ch, LANES), BF16)
@@ -139,50 +134,64 @@
     ccol = lane_iota(chunk) & (side - 1)
     scale = math.log2(math.e) / math.sqrt(HEAD)
 
-    def attend(c, _):
-        base = pl.multiple_of(c * chunk, chunk)
+    def lift(base):
         lifted = dot(t_in[...], patch[:, pl.ds(base, chunk)])
+        att[:, pl.ds(base, chunk)] = lifted
         normed = norm_channels(lifted).astype(BF16)
         windows = dot(normed, perm[...]).astype(BF16)
-        qkv = dot(t_qkv[...], windows).astype(BF16)
-        mixed = []
-        for h in range(heads):
-            parts = []
-            for p in range(chunk // LANES):
-                def piece(kind):
-                    top = kind * hid + h * HEAD
-                    return qkv[top : top + HEAD, p * LANES : (p + 1) * LANES]
-                scores = dot_tn(piece(1), piece(0))
-                scores = jnp.where(low, scores[:win_cells], scores[win_cells:])
-                top = jnp.max(scores, axis=0, keepdims=True)
-                raised = jnp.exp2((scores - top) * scale)
+        qkv_ref[:, pl.ds(base, chunk)] = dot(t_qkv[...], windows).astype(BF16)
+
+    head_of = lax.broadcasted_iota(jnp.int32, (1, hid), 1) < HEAD
+    zero = jnp.zeros((HEAD, LANES), BF16)
+
+    def attend(base):
+        tiles = [pl.ds(pl.multiple_of(base + p * LANES, LANES), LANES) for p in range(chunk // LANES)]
+        scores = []
+        for at in tiles:
+            keys = qkv_ref[hid : 2 * hid, at].T
+            both = jnp.concatenate(
+                [jnp.where(head_of, keys, 0), jnp.where(head_of, 0, keys)], axis=0
+            ).astype(BF16)
+            scores.append(dot(both, qkv_ref[:hid, at]))
+        spreads = []
+        for full in scores:
+            spread = []
+            for h in range(heads):
+                top = h * LANES
+                own = jnp.where(low, full[top : top + win_cells], full[top + win_cells : top + LANES])
+                most = jnp.max(own, axis=0, keepdims=True)
+                raised = jnp.exp2((own - most) * scale)
                 total = jnp.sum(raised, axis=0, keepdims=True)
                 probs = raised * (1.0 / total)
-                spread = jnp.concatenate(
-                    [jnp.where(low, probs, 0.0), jnp.where(low, 0.0, probs)], axis=0
-                ).astype(BF16)
-                parts.append(dot(piece(2), spread))
-            mixed.append(jnp.concatenate(parts, axis=1))
-        mixed = jnp.concatenate(mixed, axis=0).astype(BF16)
-        mixed = dot(mixed, perm[...]).astype(BF16)
-        attended = lifted + dot(t_proj[...], mixed)
+                spread += [jnp.where(low, probs, 0.0), jnp.where(low, 0.0, probs)]
+            spreads.append(jnp.concatenate(spread, axis=0).astype(BF16))
+        for at, spread in zip(tiles, spreads):
+            values = jnp.concatenate(
+                [
+                    jnp.concatenate([qkv_ref[2 * hid : 2 * hid + HEAD, at], zero], axis=1),
+                    jnp.concatenate([zero, qkv_ref[2 * hid + HEAD :, at]], axis=1),
+                ],
+                axis=0,
+            )
+            mixed_ref[:, at] = dot(values, spread).astype(BF16)
+
+    def project(base):
+        mixed = dot(mixed_ref[:, pl.ds(base, chunk)], perm[...]).astype(BF16)
+        attended = att[:, pl.ds(base, chunk)] + dot(t_proj[...], mixed)
         att[:, pl.ds(base, chunk)] = attended
-        conv_in = norm_channels(attended)
-        left = jnp.where(ccol > 0, pltpu.roll(conv_in, 1, 1), 0.0)
-        right = jnp.where(ccol < side - 1, pltpu.roll(conv_in, chunk - 1, 1), 0.0)
+        conv_in = norm_channels(attended).astype(BF16)
+        left = jnp.where(ccol > 0, pltpu.roll(conv_in, 1, 1), 0)
+        right = jnp.where(ccol < side - 1, pltpu.roll(conv_in, chunk - 1, 1), 0)
         here = pl.ds(pl.multiple_of(base + LANES, LANES), chunk)
         even[:hid, here] = left.astype(BF16)
-        even[hid : 2 * hid, here] = conv_in.astype(BF16)
+        even[hid : 2 * hid, here] = conv_in
         even[2 * hid :, here] = right.astype(BF16)
+
+    def shift(base):
         around = even[:, pl.ds(base, chunk + LANES)]
         odd[:, pl.ds(base, chunk)] = around[:, side : side + chunk]
-        return 0
-
-    lax.fori_loop(0, chunks, attend, 0)
-    odd[:, cells:] = even[:, cells : cells + 2 * LANES][:, side : side + LANES]
-
-    def finish(c, _):
-        base = pl.multiple_of(c * chunk, chunk)
+
+    def finish(base):
         after = pl.ds(pl.multiple_of(base + LANES, LANES), chunk)
         around = jnp.concatenate(
             [odd[:, pl.ds(base, chunk)], even[:, after], odd[:, after]], axis=0
@@ -192,9 +201,18 @@
         expanded = silu(dot(t_up[...], mlp_in)).astype(BF16)
         finished = convolved + dot(t_down[...], expanded)
         taps[:, pl.ds(base, chunk)] = dot(w_out[...], finished.astype(BF16))
-        return 0
-
-    lax.fori_loop(0, chunks, finish, 0)
+
+    for c in range(chunks):
+        lift(c * chunk)
+    for c in range(chunks):
+        attend(c * chunk)
+    for c in range(chunks):
+        project(c * chunk)
+    for c in range(chunks):
+        shift(c * chunk)
+    odd[:, cells:] = even[:, cells : cells + 2 * LANES][:, side : side + LANES]
+    for c in range(chunks):
+        finish(c * chunk)
 
     delta = jnp.zeros((ch, cells), F32)
     for t, (dy, dx) in enumerate(offsets):
@@ -212,53 +230,68 @@
         out_ref[b, pieces * ch :, :] = note[:META, :]
 
 
-def refine_tiles(tiles, weights, bands):
-    count, ch, width = tiles.shape
+def refine_tiles(order, tiles, weights, bands, before=None):
+    _, ch, width = tiles.shape
     cells = width - LANES
     side = math.isqrt(cells)
-    w_in, w_qkv, w_proj, w_mid, w_up, w_down, w_out = weights
-    hid = w_proj.shape[0]
-    mlp = w_up.shape[1]
-    w_in = w_in.reshape(-1, hid)
-    w_mid = w_mid.reshape(-1, hid)
-    w_out = jnp.swapaxes(w_out, 2, 3).reshape(-1, hid)
+    first = before is None
+    if first:
+        w_in, w_qkv, w_proj, w_mid, w_up, w_down, w_out = weights
+        hid = w_proj.shape[0]
+        w_in = w_in.reshape(-1, hid)
+        w_mid = w_mid.reshape(-1, hid)
+        w_out = jnp.swapaxes(w_out, 2, 3).reshape(-1, hid)
+        operands = (w_in, w_qkv, w_proj, w_mid, w_up, w_down, w_out)
+        chunk = WIN * side
+        flipped = [jax.ShapeDtypeStruct(w.shape[::-1], BF16) for w in operands[:-1]]
+        flipped.append(jax.ShapeDtypeStruct((chunk, chunk), BF16))
+    else:
+        chunks, w_out, *rest = before
+        operands = (chunks, w_out, *rest)
+        hid = w_out.shape[1]
+        flipped = []
     taps = w_out.shape[0]
-    chunk = WIN * side
     rows = (cells // bands + 2 * LANES) // LANES * ch + META
     whole = pl.BlockSpec(memory_space=pltpu.VMEM)
-    return pl.pallas_call(
-        functools.partial(refine_kernel, side=side, bands=bands),
-        out_shape=jax.ShapeDtypeStruct((count * bands, rows, LANES), BF16),
-        grid=(count,),
-        in_specs=[pl.BlockSpec((1, ch, width), lambda i: (i, 0, 0))] + [whole] * 7,
-        out_specs=pl.BlockSpec((bands, rows, LANES), lambda i: (i, 0, 0)),
-        scratch_shapes=[
-            pltpu.VMEM((hid, w_in.shape[0]), BF16),
-            pltpu.VMEM((3 * hid, hid), BF16),
-            pltpu.VMEM((hid, hid), BF16),
-            pltpu.VMEM((hid, w_mid.shape[0]), BF16),
-            pltpu.VMEM((mlp, hid), BF16),
-            pltpu.VMEM((hid, mlp), BF16),
-            pltpu.VMEM((chunk, chunk), BF16),
-            pltpu.VMEM((w_in.shape[0], cells), BF16),
-            pltpu.VMEM((hid, cells), F32),
-            pltpu.VMEM((3 * hid, cells + 2 * LANES), BF16),
-            pltpu.VMEM((3 * hid, cells + LANES), BF16),
-            pltpu.VMEM((taps, cells), F32),
-            pltpu.VMEM((ch, cells + 2 * LANES), BF16),
-        ],
+    in_specs = [pl.BlockSpec((1, ch, width), lambda i, o: (o[i], 0, 0))]
+    in_specs += [whole if first else pl.BlockSpec(memory_space=pl.ANY)] + [whole] * (len(operands) - 1)
+    steps = order.shape[0]
+    results = pl.pallas_call(
+        functools.partial(refine_kernel, side=side, bands=bands, first=first),
+        out_shape=[jax.ShapeDtypeStruct((tiles.shape[0] * bands, rows, LANES), BF16)] + flipped,
+        grid_spec=pltpu.PrefetchScalarGridSpec(
+            num_scalar_prefetch=1,
+            grid=(steps,),
+            in_specs=in_specs,
+            out_specs=[pl.BlockSpec((bands, rows, LANES), lambda i, o: (o[i], 0, 0))]
+            + [whole] * len(flipped),
+            scratch_shapes=[
+                pltpu.VMEM((taps, cells), BF16),
+                pltpu.VMEM((hid, cells), F32),
+                pltpu.VMEM((3 * hid, cells + 2 * LANES), BF16),
+                pltpu.VMEM((3 * hid, cells + LANES), BF16),
+                pltpu.VMEM((taps, cells), F32),
+                pltpu.VMEM((ch, cells + 2 * LANES), BF16),
+                pltpu.VMEM((3 * hid, cells), BF16),
+                pltpu.VMEM((hid, cells), BF16),
+            ],
+        ),
+        input_output_aliases={} if first else {2: 0},
         compiler_params=pltpu.CompilerParams(vmem_limit_bytes=VMEM_LIMIT),
-        name="refine",
-    )(tiles, w_in, w_qkv, w_proj, w_mid, w_up, w_down, w_out)
+        cost_estimate=pl.CostEstimate(
+            flops=steps * 4 * 10**9, bytes_accessed=steps * 2**21, transcendentals=steps * 3 * 10**6
+        ),
+        name="refine_own" if first else "refine_rest",
+    )(order, tiles, *operands)
+    return [results[0], w_out, *results[1:]] if first else results[0]
 
 
 def decode_kernel(
     where_ref, pieces_ref, w_in, w_mid, out_ref, t_in, t_mid, strip, act, rows_out,
     *, groups, lanes_in_strip, side,
 ):
-    frames, _, ch3, cols = strip.shape
+    frames, _, _, cols = strip.shape
     frames -= 2
-    ch = pieces_ref.shape[1] * 0 + ch3
     frame = pl.program_id(0)
     band = out_ref.shape[2]
     dec = out_ref.shape[1]
@@ -320,20 +353,22 @@
             axis=0,
         )
         value = silu(dot(t_in[...], around))
-        outside = (first_row & (y == 0)) | (last_row & (y == band + 1))
-        value = jnp.where(outside, 0.0, value)
-        left = jnp.where(col > 0, pltpu.roll(value, 1, 1), 0.0)
-        right = jnp.where(col < cols - 1, pltpu.roll(value, cols - 1, 1), 0.0)
-        base = pl.multiple_of(y * 3 * dec, 3 * dec)
-        act[pl.ds(base, dec), :] = left.astype(BF16)
-        act[pl.ds(base + dec, dec), :] = value.astype(BF16)
-        act[pl.ds(base + 2 * dec, dec), :] = right.astype(BF16)
+        if y == 0:
+            value = jnp.where(first_row, 0.0, value)
+        if y == band + 1:
+            value = jnp.where(last_row, 0.0, value)
+        value = value.astype(BF16)
+        left = jnp.where(col > 0, pltpu.roll(value, 1, 1), 0).astype(BF16)
+        right = jnp.where(col < cols - 1, pltpu.roll(value, cols - 1, 1), 0).astype(BF16)
+        base = y * 3 * dec
+        act[pl.ds(base, dec), :] = left
+        act[pl.ds(base + dec, dec), :] = value
+        act[pl.ds(base + 2 * dec, dec), :] = right
         return 0
 
-    lax.fori_loop(0, band + 2, act_row, 0)
 
     def out_row(y, _):
-        base = pl.multiple_of(y * 3 * dec, 3 * dec)
+        base = y * 3 * dec
         value = dot(t_mid[...], act[pl.ds(base, 9 * dec), :])
         value = value + act[pl.ds(base + 4 * dec, dec), :].astype(F32)
         for k in range(cols // LANES):
@@ -342,7 +377,10 @@
             ]
         return 0
 
-    lax.fori_loop(0, band, out_row, 0)
+    for y in range(band + 2):
+        act_row(y, 0)
+    for y in range(band):
+        out_row(y, 0)
     for k in range(cols // LANES):
         done = rows_out[k * dec * band : (k + 1) * dec * band, :]
         out_ref[0, :, :, k * LANES : (k + 1) * LANES] = done.reshape(dec, band, LANES).astype(BF16)
@@ -386,7 +424,9 @@
     outgoing = pick_tiles(tile_routes.reshape(-1), own_tiles, groups)
     landing = lax.all_to_all(outgoing, "pool", split_axis=0, concat_axis=0, tiled=True)
     weights = (w_in[0], w_qkv[0], w_proj[0], w_mid[0], w_up[0], w_down[0], w_out[0])
-    chunks = refine_tiles(landing, weights, columns)
+    order = (lax.axis_index("pool") + jnp.arange(groups, dtype=jnp.int32)) % groups
+    done = refine_tiles(order[:1], outgoing, weights, columns)
+    chunks = refine_tiles(order[1:], landing, None, columns, done)
     pieces = lax.all_to_all(chunks, ("pool", "dev"), split_axis=0, concat_axis=0, tiled=True)
     where = jnp.stack([lax.axis_index("dev"), jnp.int32(columns)])
     return decode_band(where, pieces, dec_in, dec_mid, frames, groups, columns, side)[None]

time: 232 us -> 138 us (0.59)
  Pallas kernels: 188 us -> 100 us
  blocking collectives: 14.8 us -> 0 us
  starting transfers between devices: 4.2 us -> 11.5 us
    pallas_call x1 -> x2, Pallas kernels: 140 us -> 71.6 us  [refine_tiles(): pl.pallas_call(functools.partial(refine_kernel, side=side, bands=bands, f...]
    pallas_call x1, Pallas kernels: 44.1 us -> 26.5 us  [decode_band(): pl.pallas_call(functools.partial(decode_kernel, groups=groups, lanes_in_s...]
    all_to_all x1 -> x0, blocking collectives: 14.8 us -> none  [shards(): lax.all_to_all(outgoing, 'pool', split_axis=0, concat_axis=0, tiled=True)]
    all_to_all x0 -> x1, starting transfers between devices: none -> 5.19 us  [shards(): lax.all_to_all(outgoing, 'pool', split_axis=0, concat_axis=0, tiled=True)]
  transfers between devices with their start and end apart: 1 -> 2, of which waited for: 1 -> 1; matrix products, arithmetic and copies ran while one was open for 0% -> 1% of each run, Pallas kernels for 0% -> 14%
where the time goes in v1:
time: 138 us; the launch traced here: 137 us
  Pallas kernels  100 us (72%)
  waiting for transfers between devices  22.6 us (16%)
  starting transfers between devices  11.5 us (8%)
  local copies, waits for them, and re-layouts  2.36 us (2%)
    pallas_call x2, Pallas kernels, refine_tiles(): pl.pallas_call(functools.partial(refine_kernel, side=side, bands=bands, f...  71.6 us
    pallas_call x1, Pallas kernels, decode_band(): pl.pallas_call(functools.partial(decode_kernel, groups=groups, lanes_in_s...  26.5 us
    all_to_all x1, waiting for transfers between devices, shards(): lax.all_to_all(chunks, ('pool', 'dev'), split_axis=0, concat_axis=0, tile...  22.6 us
    all_to_all x1, starting transfers between devices, shards(): lax.all_to_all(chunks, ('pool', 'dev'), split_axis=0, concat_axis=0, tile...  6.35 us
    all_to_all x1, starting transfers between devices, shards(): lax.all_to_all(outgoing, 'pool', split_axis=0, concat_axis=0, tiled=True)  5.19 us
  transfers between devices with their start and end apart: 2, of which 1 were waited for; matrix products, arithmetic and copies ran while one was open for 1% of the time, Pallas kernels for 14%

profile of v1, /device:TPU:0, one launch (start us, length us, event | category | flops | bytes accessed | tf_op | source)
XLA Modules:
  0.0 137.2 jit_solution(2784665282999679353)
XLA Ops:
  0.0 1.9 %pick.1.refs_1_ = bf16[4,16,4224]{2,1,0:T(8,128)(2,1)} custom-call(s32[4]{0:T(128)} %bitcast.21, bf16[4,16,4096]{2,1,0:T(8,128)(2,1)} %bitcast.19), custom_call_target="tpu_custom_call" | custom-call | tf_op jit(solution)/shard_map/pick/pallas_call | solution.py:62
  1.9 5.2 %all-to-all-start = ((bf16[4,16,4224]{2,1,0:T(8,128)(2,1)}), bf16[4,16,4224]{2,1,0:T(8,128)(2,1)S(1)}, u32[]{:S(2)}, u32[]{:S(2)}) async-start(bf16[4,16,4224]{2,1,0:T(8,128)(2,1)} %pick.1.refs_1_), calls=%async_computation | async-start | bytes 1081344 | tf_op jit(solution)/shard_map/all_to_all | solution.py:425
  7.1 0.0 copy-start.2
  7.1 0.7 slice.6.refs_0_
  7.8 0.0 copy-done.2
  7.8 19.2 %refine_own.1 = (bf16[32,104,128]{2,1,0:T(8,128)(2,1)}, bf16[128,144]{1,0:T(8,128)(2,1)}, bf16[384,128]{1,0:T(8,128)(2,1)}, bf16[128,128]{1,0:T(8,128)(2,1)}, bf...) custom-call(s32[1]{0:T(128)} %bitcast.30, ...), custom_call_target="tpu_custom_call" | custom-call | flops 4000000000 | bytes 2097152 | tf_op jit(solution)/shard_map/refine_own/pallas_call | solution.py:259
  27.0 0.0 all-to-all-done.refs_1_
  27.0 0.0 copy-start.1
  27.0 0.8 copy-done.1
  27.8 52.4 %refine_rest.1 = bf16[32,104,128]{2,1,0:T(8,128)(2,1)} custom-call(s32[3]{0:T(128)} %slice.6.refs_0_, bf16[4,16,4224]{2,1,0:T(8,128)(2,1)} %copy-done.1, bf16[32,104,128]{2,1,0:T(8,128)(2,1)} %get-tuple-element.13.refs_2_, bf16[144,128]{1,0:T(8,128)(2,1)} %bitcast.28, bf16[128,144]{1,0:T(8,128)(2,1)} %get-tuple-element.14.refs_4_, ...), custom_call_target="tpu_custom_call", output_to_operand_aliasing={{}: (2, {})} | custom-call | flops 12000000000 | bytes 6291456 | tf_op jit(solution)/shard_map/refine_rest/pallas_call | solution.py:259
  80.1 6.3 %all-to-all-start.1 = ((bf16[32,104,128]{2,1,0:T(8,128)(2,1)}), bf16[32,104,128]{2,1,0:T(8,128)(2,1)S(1)}, u32[]{:S(2)}, u32[]{:S(2)}) async-start(bf16[32,104,128]{2,1,0:T(8,128)(2,1)} %refine_rest.1), calls=%async_computation.1 | async-start | bytes 1703936 | tf_op jit(solution)/shard_map/all_to_all | solution.py:430
  86.5 0.7 pad_add_fusion.where_ref
  87.2 22.6 %all-to-all-done.1.pieces_ref = bf16[32,104,128]{2,1,0:T(8,128)(2,1)S(1)} async-done(((bf16[32,104,128]{2,1,0:T(8,128)(2,1)}), bf16[32,104,128]{2,1,0:T(8,128)(2,1)S(1)}, u32[]{:S(2)}, u32[]{:S(2)}) %all-to-all-start.1) | async-done | bytes 852000 | tf_op jit(solution)/shard_map/all_to_all | solution.py:430
  109.8 0.0 copy-start
  109.8 0.9 copy-done
  110.7 26.5 %decode.1 = bf16[4,192,8,512]{3,2,1,0:T(8,128)(2,1)} custom-call(s32[2]{0:T(128)} %pad_add_fusion.where_ref, bf16[32,104,128]{2,1,0:T(8,128)(2,1)} %copy-done, bf16[432,192]{1,0:T(8,128)(2,1)} %bitcast.20, bf16[1728,192]{1,0:T(8,128)(2,1)} %bitcast.18), custom_call_target="tpu_custom_call" | custom-call | tf_op jit(solution)/shard_map/decode/pallas_call | solution.py:397
  (1 shorter events, 0.0 us)
Async XLA Ops:
  1.9 25.0 %all-to-all-start = ((bf16[4,16,4224]{2,1,0:T(8,128)(2,1)}), bf16[4,16,4224]{2,1,0:T(8,128)(2,1)S(1)}, u32[]{:S(2)}, u32[]{:S(2)}) async-start(bf16[4,16,4224]{2,1,0:T(8,128)(2,1)} %pick.1.refs_1_), calls=%async_computation | async-start | bytes 1081344 | tf_op jit(solution)/shard_map/all_to_all | solution.py:425
  7.1 0.7 copy-start.2
  27.0 0.8 copy-start.1
  80.1 29.6 %all-to-all-start.1 = ((bf16[32,104,128]{2,1,0:T(8,128)(2,1)}), bf16[32,104,128]{2,1,0:T(8,128)(2,1)S(1)}, u32[]{:S(2)}, u32[]{:S(2)}) async-start(bf16[32,104,128]{2,1,0:T(8,128)(2,1)} %refine_rest.1), calls=%async_computation.1 | async-start | bytes 1703936 | tf_op jit(solution)/shard_map/all_to_all | solution.py:430
  109.8 0.9 copy-start

commit v2 on v1

--- a/solution.py
+++ b/solution.py
@@ -77,7 +77,7 @@
         _, tile_ref, _, w_out, t_in, t_qkv, t_proj, t_mid, t_up, t_down, perm = refs[:11]
         out_ref = refs[11]
         scratch = refs[12:]
-    patch, att, even, odd, taps, padded, qkv_ref, mixed_ref = scratch
+    patch, att, even, odd, taps, padded, qkv_ref, mixed_ref, wide, wide_f = scratch
     ch = tile_ref.shape[1]
     cells = side * side
     hid = t_proj.shape[0]
@@ -137,35 +137,47 @@
     def lift(base):
         lifted = dot(t_in[...], patch[:, pl.ds(base, chunk)])
         att[:, pl.ds(base, chunk)] = lifted
-        normed = norm_channels(lifted).astype(BF16)
-        windows = dot(normed, perm[...]).astype(BF16)
-        qkv_ref[:, pl.ds(base, chunk)] = dot(t_qkv[...], windows).astype(BF16)
+        mixed_ref[:, pl.ds(base, chunk)] = norm_channels(lifted).astype(BF16)
+
+    def lift2(base):
+        mixed_ref[:, pl.ds(base, chunk)] = dot(mixed_ref[:, pl.ds(base, chunk)], perm[...]).astype(BF16)
+
+    def lift3(base):
+        qkv_ref[:, pl.ds(base, chunk)] = dot(t_qkv[...], mixed_ref[:, pl.ds(base, chunk)]).astype(BF16)
 
     head_of = lax.broadcasted_iota(jnp.int32, (1, hid), 1) < HEAD
     zero = jnp.zeros((HEAD, LANES), BF16)
 
     def attend(base):
-        tiles = [pl.ds(pl.multiple_of(base + p * LANES, LANES), LANES) for p in range(chunk // LANES)]
-        scores = []
-        for at in tiles:
+        for p in range(chunk // LANES):
+            at = pl.ds(base + p * LANES, LANES)
             keys = qkv_ref[hid : 2 * hid, at].T
             both = jnp.concatenate(
                 [jnp.where(head_of, keys, 0), jnp.where(head_of, 0, keys)], axis=0
             ).astype(BF16)
-            scores.append(dot(both, qkv_ref[:hid, at]))
-        spreads = []
-        for full in scores:
-            spread = []
+            full = dot(both, qkv_ref[:hid, at])
             for h in range(heads):
                 top = h * LANES
-                own = jnp.where(low, full[top : top + win_cells], full[top + win_cells : top + LANES])
+                wide_f[h * win_cells : (h + 1) * win_cells, at] = jnp.where(
+                    low, full[top : top + win_cells], full[top + win_cells : top + LANES]
+                )
+
+    def attend2(base):
+        for p in range(chunk // LANES):
+            at = pl.ds(base + p * LANES, LANES)
+            for h in range(heads):
+                own = wide_f[h * win_cells : (h + 1) * win_cells, at]
                 most = jnp.max(own, axis=0, keepdims=True)
                 raised = jnp.exp2((own - most) * scale)
                 total = jnp.sum(raised, axis=0, keepdims=True)
-                probs = raised * (1.0 / total)
-                spread += [jnp.where(low, probs, 0.0), jnp.where(low, 0.0, probs)]
-            spreads.append(jnp.concatenate(spread, axis=0).astype(BF16))
-        for at, spread in zip(tiles, spreads):
+                probs = (raised * (1.0 / total)).astype(BF16)
+                top = h * LANES
+                wide[top : top + win_cells, at] = jnp.where(low, probs, 0)
+                wide[top + win_cells : top + LANES, at] = jnp.where(low, 0, probs)
+
+    def attend3(base):
+        for p in range(chunk // LANES):
+            at = pl.ds(base + p * LANES, LANES)
             values = jnp.concatenate(
                 [
                     jnp.concatenate([qkv_ref[2 * hid : 2 * hid + HEAD, at], zero], axis=1),
@@ -173,46 +185,56 @@
                 ],
                 axis=0,
             )
-            mixed_ref[:, at] = dot(values, spread).astype(BF16)
+            mixed_ref[:, at] = dot(values, wide[: heads * LANES, at]).astype(BF16)
 
     def project(base):
-        mixed = dot(mixed_ref[:, pl.ds(base, chunk)], perm[...]).astype(BF16)
-        attended = att[:, pl.ds(base, chunk)] + dot(t_proj[...], mixed)
+        mixed_ref[:, pl.ds(base, chunk)] = dot(mixed_ref[:, pl.ds(base, chunk)], perm[...]).astype(BF16)
+
+    def project2(base):
+        attended = att[:, pl.ds(base, chunk)] + dot(t_proj[...], mixed_ref[:, pl.ds(base, chunk)])
         att[:, pl.ds(base, chunk)] = attended
-        conv_in = norm_channels(attended).astype(BF16)
-        left = jnp.where(ccol > 0, pltpu.roll(conv_in, 1, 1), 0)
-        right = jnp.where(ccol < side - 1, pltpu.roll(conv_in, chunk - 1, 1), 0)
-        here = pl.ds(pl.multiple_of(base + LANES, LANES), chunk)
-        even[:hid, here] = left.astype(BF16)
-        even[hid : 2 * hid, here] = conv_in
-        even[2 * hid :, here] = right.astype(BF16)
+        here = pl.ds(base + LANES, chunk)
+        even[hid : 2 * hid, here] = norm_channels(attended).astype(BF16)
+
+    def project3(base):
+        here = pl.ds(base + LANES, chunk)
+        conv_in = even[hid : 2 * hid, here]
+        even[:hid, here] = jnp.where(ccol > 0, pltpu.roll(conv_in, 1, 1), 0)
+        even[2 * hid :, here] = jnp.where(ccol < side - 1, pltpu.roll(conv_in, chunk - 1, 1), 0)
 
     def shift(base):
         around = even[:, pl.ds(base, chunk + LANES)]
         odd[:, pl.ds(base, chunk)] = around[:, side : side + chunk]
 
-    def finish(base):
-        after = pl.ds(pl.multiple_of(base + LANES, LANES), chunk)
+    def finish1(base):
+        after = pl.ds(base + LANES, chunk)
         around = jnp.concatenate(
             [odd[:, pl.ds(base, chunk)], even[:, after], odd[:, after]], axis=0
         )
         convolved = att[:, pl.ds(base, chunk)] + silu(dot(t_mid[...], around))
-        mlp_in = norm_channels(convolved).astype(BF16)
-        expanded = silu(dot(t_up[...], mlp_in)).astype(BF16)
-        finished = convolved + dot(t_down[...], expanded)
-        taps[:, pl.ds(base, chunk)] = dot(w_out[...], finished.astype(BF16))
-
-    for c in range(chunks):
-        lift(c * chunk)
-    for c in range(chunks):
-        attend(c * chunk)
-    for c in range(chunks):
-        project(c * chunk)
-    for c in range(chunks):
-        shift(c * chunk)
-    odd[:, cells:] = even[:, cells : cells + 2 * LANES][:, side : side + LANES]
-    for c in range(chunks):
-        finish(c * chunk)
+        att[:, pl.ds(base, chunk)] = convolved
+        mixed_ref[:, pl.ds(base, chunk)] = norm_channels(convolved).astype(BF16)
+
+    def finish2(base):
+        wide[:, pl.ds(base, chunk)] = silu(dot(t_up[...], mixed_ref[:, pl.ds(base, chunk)])).astype(BF16)
+
+    def finish3(base):
+        finished = att[:, pl.ds(base, chunk)] + dot(t_down[...], wide[:, pl.ds(base, chunk)])
+        mixed_ref[:, pl.ds(base, chunk)] = finished.astype(BF16)
+
+    def finish4(base):
+        taps[:, pl.ds(base, chunk)] = dot(w_out[...], mixed_ref[:, pl.ds(base, chunk)])
+
+    lags = (
+        (finish4, 14), (finish3, 13), (finish2, 12), (finish1, 11), (shift, 9), (project3, 8),
+        (project2, 7), (project, 6), (attend3, 5), (attend2, 4), (attend, 3), (lift3, 2), (lift2, 1), (lift, 0),
+    )
+    for step in range(chunks + 14):
+        for body, lag in lags:
+            if 0 <= step - lag < chunks:
+                body((step - lag) * chunk)
+                if body is shift and step - lag == chunks - 1:
+                    odd[:, cells:] = even[:, cells : cells + 2 * LANES][:, side : side + LANES]
 
     delta = jnp.zeros((ch, cells), F32)
     for t, (dy, dx) in enumerate(offsets):
@@ -245,10 +267,12 @@
         chunk = WIN * side
         flipped = [jax.ShapeDtypeStruct(w.shape[::-1], BF16) for w in operands[:-1]]
         flipped.append(jax.ShapeDtypeStruct((chunk, chunk), BF16))
+        mlp = w_up.shape[1]
     else:
         chunks, w_out, *rest = before
         operands = (chunks, w_out, *rest)
         hid = w_out.shape[1]
+        mlp = rest[4].shape[0]
         flipped = []
     taps = w_out.shape[0]
     rows = (cells // bands + 2 * LANES) // LANES * ch + META
@@ -274,6 +298,8 @@
                 pltpu.VMEM((ch, cells + 2 * LANES), BF16),
                 pltpu.VMEM((3 * hid, cells), BF16),
                 pltpu.VMEM((hid, cells), BF16),
+                pltpu.VMEM((mlp, cells), BF16),
+                pltpu.VMEM((hid, cells), F32),
             ],
         ),
         input_output_aliases={} if first else {2: 0},
@@ -287,7 +313,7 @@
 
 
 def decode_kernel(
-    where_ref, pieces_ref, w_in, w_mid, out_ref, t_in, t_mid, strip, act, rows_out,
+    where_ref, pieces_ref, t_in, t_mid, out_ref, strip, act, rows_out,
     *, groups, lanes_in_strip, side,
 ):
     frames, _, _, cols = strip.shape
@@ -296,7 +322,7 @@
     band = out_ref.shape[2]
     dec = out_ref.shape[1]
     tall = band + 4
-    ch = w_in.shape[0] // 27
+    ch = t_in.shape[1] // 27
     columns = lanes_in_strip
     lane = lane_iota(LANES)
     low = lane < side
@@ -304,8 +330,6 @@
 
     @pl.when(frame == 0)
     def _():
-        t_in[...] = w_in[...].astype(F32).T.astype(BF16)
-        t_mid[...] = w_mid[...].astype(F32).T.astype(BF16)
         strip[0:2] = jnp.zeros((2,) + strip.shape[1:], BF16)
         note_at = tall * side // LANES * ch
         notes = [
@@ -343,7 +367,7 @@
     first_row = where_ref[0] == 0
     last_row = where_ref[0] == where_ref[1] - 1
 
-    def act_row(y, _):
+    def act_row(y):
         around = jnp.concatenate(
             [
                 strip[pl.ds(frame + dt, 1), pl.ds(y + dy, 1)].reshape(3 * ch, cols)
@@ -357,43 +381,62 @@
             value = jnp.where(first_row, 0.0, value)
         if y == band + 1:
             value = jnp.where(last_row, 0.0, value)
-        value = value.astype(BF16)
-        left = jnp.where(col > 0, pltpu.roll(value, 1, 1), 0).astype(BF16)
-        right = jnp.where(col < cols - 1, pltpu.roll(value, cols - 1, 1), 0).astype(BF16)
-        base = y * 3 * dec
-        act[pl.ds(base, dec), :] = left
-        act[pl.ds(base + dec, dec), :] = value
-        act[pl.ds(base + 2 * dec, dec), :] = right
-        return 0
-
-
-    def out_row(y, _):
-        base = y * 3 * dec
-        value = dot(t_mid[...], act[pl.ds(base, 9 * dec), :])
-        value = value + act[pl.ds(base + 4 * dec, dec), :].astype(F32)
+        top = y * 3 * dec
+        act[top + dec : top + 2 * dec, :] = value.astype(BF16)
+
+    def side_rows(y):
+        top = y * 3 * dec
+        value = act[top + dec : top + 2 * dec, :]
+        act[top : top + dec, :] = jnp.where(col > 0, pltpu.roll(value, 1, 1), 0)
+        act[top + 2 * dec : top + 3 * dec, :] = jnp.where(
+            col < cols - 1, pltpu.roll(value, cols - 1, 1), 0
+        )
+
+    def out_row(y):
+        top = y * 3 * dec
+        value = dot(t_mid[...], act[top : top + 9 * dec, :])
+        value = value + act[top + 4 * dec : top + 5 * dec, :].astype(F32)
         for k in range(cols // LANES):
             rows_out[pl.ds(k * dec * band + y, dec, stride=band), :] = value[
                 :, k * LANES : (k + 1) * LANES
             ]
-        return 0
 
     for y in range(band + 2):
-        act_row(y, 0)
+        act_row(y)
+    for y in range(band + 2):
+        side_rows(y)
     for y in range(band):
-        out_row(y, 0)
+        out_row(y)
     for k in range(cols // LANES):
         done = rows_out[k * dec * band : (k + 1) * dec * band, :]
         out_ref[0, :, :, k * LANES : (k + 1) * LANES] = done.reshape(dec, band, LANES).astype(BF16)
 
 
-def decode_band(where, pieces, dec_in, dec_mid, frames, groups, columns, side):
-    ch, dec = dec_in.shape[3:]
+def flip_kernel(w_in, w_mid, t_in, t_mid):
+    t_in[...] = w_in[...].astype(F32).T.astype(BF16)
+    t_mid[...] = w_mid[...].astype(F32).T.astype(BF16)
+
+
+def flip_weights(dec_in, dec_mid):
+    dec = dec_in.shape[-1]
+    both = (dec_in.reshape(-1, dec), dec_mid.reshape(-1, dec))
+    return pl.pallas_call(
+        flip_kernel,
+        out_shape=[jax.ShapeDtypeStruct(w.shape[::-1], BF16) for w in both],
+        in_specs=[pl.BlockSpec(memory_space=pltpu.VMEM)] * 2,
+        out_specs=[pl.BlockSpec(memory_space=pltpu.VMEM)] * 2,
+        cost_estimate=pl.CostEstimate(flops=10**6, bytes_accessed=2**21, transcendentals=0),
+        name="flip",
+    )(*both)
+
+
+def decode_band(where, pieces, t_in, t_mid, frames, groups, columns, side):
+    dec = t_in.shape[0]
+    ch = t_in.shape[1] // 27
     count, rows, _ = pieces.shape
     band = (rows - META) // ch * LANES // side - 4
     cols = columns * side
     whole = pl.BlockSpec(memory_space=pltpu.VMEM)
-    w_in = dec_in.reshape(-1, dec)
-    w_mid = dec_mid.reshape(-1, dec)
     return pl.pallas_call(
         functools.partial(decode_kernel, groups=groups, lanes_in_strip=columns, side=side),
         out_shape=jax.ShapeDtypeStruct((frames, dec, band, cols), BF16),
@@ -403,8 +446,6 @@
             in_specs=[whole, whole, whole],
             out_specs=pl.BlockSpec((1, dec, band, cols), lambda f, w: (f, 0, 0, 0)),
             scratch_shapes=[
-                pltpu.VMEM((dec, w_in.shape[0]), BF16),
-                pltpu.VMEM((dec, w_mid.shape[0]), BF16),
                 pltpu.VMEM((frames + 2, band + 4, 3 * ch, cols), BF16),
                 pltpu.VMEM(((band + 2) * 3 * dec, cols), BF16),
                 pltpu.VMEM((cols // LANES * dec * band, LANES), F32),
@@ -412,7 +453,7 @@
         ),
         compiler_params=pltpu.CompilerParams(vmem_limit_bytes=VMEM_LIMIT),
         name="decode",
-    )(where, pieces, w_in, w_mid)
+    )(where, pieces, t_in, t_mid)
 
 
 def shards(latent, tile_routes, w_in, w_qkv, w_proj, w_mid, w_up, w_down, w_out, dec_in, dec_mid):
@@ -429,7 +470,9 @@
     chunks = refine_tiles(order[1:], landing, None, columns, done)
     pieces = lax.all_to_all(chunks, ("pool", "dev"), split_axis=0, concat_axis=0, tiled=True)
     where = jnp.stack([lax.axis_index("dev"), jnp.int32(columns)])
-    return decode_band(where, pieces, dec_in, dec_mid, frames, groups, columns, side)[None]
+    return decode_band(
+        where, pieces, *flip_weights(dec_in, dec_mid), frames, groups, columns, side
+    )[None]
 
 
 def solution(mesh):

time: 138 us -> 110 us (0.80)
  Pallas kernels: 100 us -> 74.8 us
  waiting for transfers between devices: 22.6 us -> 19.9 us
    pallas_call x2, Pallas kernels: 71.6 us -> 44.3 us  [refine_tiles(): pl.pallas_call(functools.partial(refine_kernel, side=side, bands=bands, f...]
    all_to_all x1, waiting for transfers between devices: 22.6 us -> 19.9 us  [shards(): lax.all_to_all(chunks, ('pool', 'dev'), split_axis=0, concat_axis=0, tile...]
    pallas_call x0 -> x1, Pallas kernels: none -> 2.54 us  [flip_weights(): pl.pallas_call(flip_kernel, out_shape=[jax.ShapeDtypeStruct(w.shape[::-1]...]
where the time goes in v2:
time: 110 us; the launch traced here: 109 us
  Pallas kernels  74.8 us (68%)
  waiting for transfers between devices  19.9 us (18%)
  starting transfers between devices  11.7 us (11%)
  local copies, waits for them, and re-layouts  2.31 us (2%)
    pallas_call x2, Pallas kernels, refine_tiles(): pl.pallas_call(functools.partial(refine_kernel, side=side, bands=bands, f...  44.3 us
    pallas_call x1, Pallas kernels, decode_band(): pl.pallas_call(functools.partial(decode_kernel, groups=groups, lanes_in_s...  26.1 us
    all_to_all x1, waiting for transfers between devices, shards(): lax.all_to_all(chunks, ('pool', 'dev'), split_axis=0, concat_axis=0, tile...  19.9 us
    all_to_all x1, starting transfers between devices, shards(): lax.all_to_all(chunks, ('pool', 'dev'), split_axis=0, concat_axis=0, tile...  6.54 us
    all_to_all x1, starting transfers between devices, shards(): lax.all_to_all(outgoing, 'pool', split_axis=0, concat_axis=0, tiled=True)  5.19 us
    pallas_call x1, Pallas kernels, flip_weights(): pl.pallas_call(flip_kernel, out_shape=[jax.ShapeDtypeStruct(w.shape[::-1]...  2.54 us
  transfers between devices with their start and end apart: 2, of which 1 were waited for; matrix products, arithmetic and copies ran while one was open for 1% of the time, Pallas kernels for 14%

profile of v2, /device:TPU:0, one launch (start us, length us, event | category | flops | bytes accessed | tf_op | source)
XLA Modules:
  0.0 109.4 jit_solution(10512884286097919668)
XLA Ops:
  0.0 1.9 %pick.1.refs_1_ = bf16[4,16,4224]{2,1,0:T(8,128)(2,1)} custom-call(s32[4]{0:T(128)} %bitcast.21, bf16[4,16,4096]{2,1,0:T(8,128)(2,1)} %bitcast.19), custom_call_target="tpu_custom_call" | custom-call | tf_op jit(solution)/shard_map/pick/pallas_call | solution.py:62
  1.9 5.2 %all-to-all-start = ((bf16[4,16,4224]{2,1,0:T(8,128)(2,1)}), bf16[4,16,4224]{2,1,0:T(8,128)(2,1)S(1)}, u32[]{:S(2)}, u32[]{:S(2)}) async-start(bf16[4,16,4224]{2,1,0:T(8,128)(2,1)} %pick.1.refs_1_), calls=%async_computation | async-start | bytes 1081344 | tf_op jit(solution)/shard_map/all_to_all | solution.py:466
  7.1 0.0 copy-start.2
  7.1 0.6 slice.6.refs_0_
  7.7 0.0 copy-done.2
  7.7 12.7 %refine_own.1 = (bf16[32,104,128]{2,1,0:T(8,128)(2,1)}, bf16[128,144]{1,0:T(8,128)(2,1)}, bf16[384,128]{1,0:T(8,128)(2,1)}, bf16[128,128]{1,0:T(8,128)(2,1)}, bf...) custom-call(s32[1]{0:T(128)} %bitcast.30, ...), custom_call_target="tpu_custom_call" | custom-call | flops 4000000000 | bytes 2097152 | tf_op jit(solution)/shard_map/refine_own/pallas_call | solution.py:283
  20.4 0.0 all-to-all-done.refs_1_
  20.4 0.0 copy-start.1
  20.4 0.8 copy-done.1
  21.2 31.6 %refine_rest.1 = bf16[32,104,128]{2,1,0:T(8,128)(2,1)} custom-call(s32[3]{0:T(128)} %slice.6.refs_0_, bf16[4,16,4224]{2,1,0:T(8,128)(2,1)} %copy-done.1, bf16[32,104,128]{2,1,0:T(8,128)(2,1)} %get-tuple-element.15.refs_2_, bf16[144,128]{1,0:T(8,128)(2,1)} %bitcast.28, bf16[128,144]{1,0:T(8,128)(2,1)} %get-tuple-element.16.refs_4_, ...), custom_call_target="tpu_custom_call", output_to_operand_aliasing={{}: (2, {})} | custom-call | flops 12000000000 | bytes 6291456 | tf_op jit(solution)/shard_map/refine_rest/pallas_call | solution.py:283
  52.8 6.5 %all-to-all-start.1 = ((bf16[32,104,128]{2,1,0:T(8,128)(2,1)}), bf16[32,104,128]{2,1,0:T(8,128)(2,1)S(1)}, u32[]{:S(2)}, u32[]{:S(2)}) async-start(bf16[32,104,128]{2,1,0:T(8,128)(2,1)} %refine_rest.1), calls=%async_computation.1 | async-start | bytes 1703936 | tf_op jit(solution)/shard_map/all_to_all | solution.py:471
  59.4 2.5 %flip.1 = (bf16[192,432]{1,0:T(8,128)(2,1)}, bf16[192,1728]{1,0:T(8,128)(2,1)}) custom-call(bf16[432,192]{1,0:T(8,128)(2,1)} %bitcast.20, bf16[1728,192]{1,0:T(8,128)(2,1)} %bitcast.18), custom_call_target="tpu_custom_call" | custom-call | flops 1000000 | bytes 2097152 | tf_op jit(solution)/shard_map/flip/pallas_call | solution.py:423
  61.9 0.6 pad_add_fusion.where_ref
  62.5 19.9 %all-to-all-done.1.pieces_ref = bf16[32,104,128]{2,1,0:T(8,128)(2,1)S(1)} async-done(((bf16[32,104,128]{2,1,0:T(8,128)(2,1)}), bf16[32,104,128]{2,1,0:T(8,128)(2,1)S(1)}, u32[]{:S(2)}, u32[]{:S(2)}) %all-to-all-start.1) | async-done | bytes 852000 | tf_op jit(solution)/shard_map/all_to_all | solution.py:471
  82.4 0.0 copy-start
  82.4 0.9 copy-done
  83.3 26.1 %decode.1 = bf16[4,192,8,512]{3,2,1,0:T(8,128)(2,1)} custom-call(s32[2]{0:T(128)} %pad_add_fusion.where_ref, bf16[32,104,128]{2,1,0:T(8,128)(2,1)} %copy-done, bf16[192,432]{1,0:T(8,128)(2,1)} %get-tuple-element.23.t_in, bf16[192,1728]{1,0:T(8,128)(2,1)} %get-tuple-element.24.t_mid), custom_call_target="tpu_custom_call" | custom-call | tf_op jit(solution)/shard_map/decode/pallas_call | solution.py:440
  (1 shorter events, 0.0 us)
Async XLA Ops:
  1.9 18.5 %all-to-all-start = ((bf16[4,16,4224]{2,1,0:T(8,128)(2,1)}), bf16[4,16,4224]{2,1,0:T(8,128)(2,1)S(1)}, u32[]{:S(2)}, u32[]{:S(2)}) async-start(bf16[4,16,4224]{2,1,0:T(8,128)(2,1)} %pick.1.refs_1_), calls=%async_computation | async-start | bytes 1081344 | tf_op jit(solution)/shard_map/all_to_all | solution.py:466
  7.1 0.6 copy-start.2
  20.4 0.8 copy-start.1
  52.8 29.6 %all-to-all-start.1 = ((bf16[32,104,128]{2,1,0:T(8,128)(2,1)}), bf16[32,104,128]{2,1,0:T(8,128)(2,1)S(1)}, u32[]{:S(2)}, u32[]{:S(2)}) async-start(bf16[32,104,128]{2,1,0:T(8,128)(2,1)} %refine_rest.1), calls=%async_computation.1 | async-start | bytes 1703936 | tf_op jit(solution)/shard_map/all_to_all | solution.py:471
  82.4 0.9 copy-start

commit v3 on v2

--- a/solution.py
+++ b/solution.py
@@ -12,6 +12,7 @@
 WIN = 8
 LANES = 128
 META = 8
+POOL = ("far", "near")
 EPS = 1e-06
 F32 = jnp.float32
 BF16 = jnp.bfloat16
@@ -252,11 +253,12 @@
         out_ref[b, pieces * ch :, :] = note[:META, :]
 
 
-def refine_tiles(order, tiles, weights, bands, before=None):
+def refine_tiles(name, place, tiles, steps, tile_at, slot_at, weights, bands, before=None):
     _, ch, width = tiles.shape
     cells = width - LANES
     side = math.isqrt(cells)
     first = before is None
+    keep = False
     if first:
         w_in, w_qkv, w_proj, w_mid, w_up, w_down, w_out = weights
         hid = w_proj.shape[0]
@@ -269,7 +271,7 @@
         flipped.append(jax.ShapeDtypeStruct((chunk, chunk), BF16))
         mlp = w_up.shape[1]
     else:
-        chunks, w_out, *rest = before
+        chunks, keep, (w_out, *rest) = before
         operands = (chunks, w_out, *rest)
         hid = w_out.shape[1]
         mlp = rest[4].shape[0]
@@ -277,17 +279,16 @@
     taps = w_out.shape[0]
     rows = (cells // bands + 2 * LANES) // LANES * ch + META
     whole = pl.BlockSpec(memory_space=pltpu.VMEM)
-    in_specs = [pl.BlockSpec((1, ch, width), lambda i, o: (o[i], 0, 0))]
+    in_specs = [pl.BlockSpec((1, ch, width), lambda i, o: (o[tile_at + i], 0, 0))]
     in_specs += [whole if first else pl.BlockSpec(memory_space=pl.ANY)] + [whole] * (len(operands) - 1)
-    steps = order.shape[0]
     results = pl.pallas_call(
         functools.partial(refine_kernel, side=side, bands=bands, first=first),
-        out_shape=[jax.ShapeDtypeStruct((tiles.shape[0] * bands, rows, LANES), BF16)] + flipped,
+        out_shape=[jax.ShapeDtypeStruct((2 * bands, rows, LANES), BF16)] + flipped,
         grid_spec=pltpu.PrefetchScalarGridSpec(
             num_scalar_prefetch=1,
             grid=(steps,),
             in_specs=in_specs,
-            out_specs=[pl.BlockSpec((bands, rows, LANES), lambda i, o: (o[i], 0, 0))]
+            out_specs=[pl.BlockSpec((bands, rows, LANES), lambda i, o: (o[slot_at + i], 0, 0))]
             + [whole] * len(flipped),
             scratch_shapes=[
                 pltpu.VMEM((taps, cells), BF16),
@@ -302,19 +303,19 @@
                 pltpu.VMEM((hid, cells), F32),
             ],
         ),
-        input_output_aliases={} if first else {2: 0},
+        input_output_aliases={2: 0} if keep else {},
         compiler_params=pltpu.CompilerParams(vmem_limit_bytes=VMEM_LIMIT),
         cost_estimate=pl.CostEstimate(
             flops=steps * 4 * 10**9, bytes_accessed=steps * 2**21, transcendentals=steps * 3 * 10**6
         ),
-        name="refine_own" if first else "refine_rest",
-    )(order, tiles, *operands)
-    return [results[0], w_out, *results[1:]] if first else results[0]
+        name=name,
+    )(place, tiles, *operands)
+    return (results[0], [w_out, *results[1:]]) if first else results[0]
 
 
 def decode_kernel(
-    where_ref, pieces_ref, t_in, t_mid, out_ref, strip, act, rows_out,
-    *, groups, lanes_in_strip, side,
+    place_ref, near_ref, far_ref, t_in, t_mid, out_ref, strip, act, rows_out,
+    *, dev_at, lanes_in_strip, side,
 ):
     frames, _, _, cols = strip.shape
     frames -= 2
@@ -324,6 +325,12 @@
     tall = band + 4
     ch = t_in.shape[1] // 27
     columns = lanes_in_strip
+    sets = [
+        [ref.at[k + d] for d in range(columns)]
+        for ref in (near_ref, far_ref)
+        for k in range(0, ref.shape[0], columns)
+    ]
+    groups = len(sets)
     lane = lane_iota(LANES)
     low = lane < side
     col = lane_iota(cols)
@@ -333,7 +340,7 @@
         strip[0:2] = jnp.zeros((2,) + strip.shape[1:], BF16)
         note_at = tall * side // LANES * ch
         notes = [
-            [pieces_ref[g * columns + d, note_at : note_at + 1, :].astype(F32) for d in range(columns)]
+            [sets[g][d][note_at : note_at + 1, :].astype(F32) for d in range(columns)]
             for g in range(groups)
         ]
         for f in range(frames):
@@ -346,7 +353,7 @@
                 for d in range(columns):
                     both.append(
                         sum(
-                            pieces_ref[g * columns + d, j * ch : (j + 1) * ch, :].astype(F32)
+                            sets[g][d][j * ch : (j + 1) * ch, :].astype(F32)
                             * picks[g][d]
                             for g in range(groups)
                         )
@@ -364,8 +371,8 @@
                     right = jnp.where(col < cols - 1, pltpu.roll(line, cols - 1, 1), 0.0)
                     strip[f + 2, y] = jnp.concatenate([left, line, right], axis=0).astype(BF16)
 
-    first_row = where_ref[0] == 0
-    last_row = where_ref[0] == where_ref[1] - 1
+    first_row = place_ref[dev_at] == 0
+    last_row = place_ref[dev_at] == cols // side - 1
 
     def act_row(y):
         around = jnp.concatenate(
@@ -430,20 +437,20 @@
     )(*both)
 
 
-def decode_band(where, pieces, t_in, t_mid, frames, groups, columns, side):
+def decode_band(place, dev_at, near, far, t_in, t_mid, frames, columns, side):
     dec = t_in.shape[0]
     ch = t_in.shape[1] // 27
-    count, rows, _ = pieces.shape
+    rows = near.shape[1]
     band = (rows - META) // ch * LANES // side - 4
     cols = columns * side
     whole = pl.BlockSpec(memory_space=pltpu.VMEM)
     return pl.pallas_call(
-        functools.partial(decode_kernel, groups=groups, lanes_in_strip=columns, side=side),
+        functools.partial(decode_kernel, dev_at=dev_at, lanes_in_strip=columns, side=side),
         out_shape=jax.ShapeDtypeStruct((frames, dec, band, cols), BF16),
         grid_spec=pltpu.PrefetchScalarGridSpec(
             num_scalar_prefetch=1,
             grid=(frames,),
-            in_specs=[whole, whole, whole],
+            in_specs=[whole] * 4,
             out_specs=pl.BlockSpec((1, dec, band, cols), lambda f, w: (f, 0, 0, 0)),
             scratch_shapes=[
                 pltpu.VMEM((frames + 2, band + 4, 3 * ch, cols), BF16),
@@ -453,41 +460,57 @@
         ),
         compiler_params=pltpu.CompilerParams(vmem_limit_bytes=VMEM_LIMIT),
         name="decode",
-    )(where, pieces, t_in, t_mid)
+    )(place, near, far, t_in, t_mid)
 
 
 def shards(latent, tile_routes, w_in, w_qkv, w_proj, w_mid, w_up, w_down, w_out, dec_in, dec_mid):
-    groups = lax.axis_size("pool")
+    halves = lax.axis_size("far")
+    pairs = lax.axis_size("near")
     columns = lax.axis_size("dev")
+    assert halves == 2 and pairs == 2
     own_tiles = latent[0]
     frames, ch, cells = own_tiles.shape
     side = math.isqrt(cells)
-    outgoing = pick_tiles(tile_routes.reshape(-1), own_tiles, groups)
-    landing = lax.all_to_all(outgoing, "pool", split_axis=0, concat_axis=0, tiled=True)
+    outgoing = pick_tiles(tile_routes.reshape(-1), own_tiles, halves * pairs)
+    landing = lax.all_to_all(outgoing, ("far", "near"), split_axis=0, concat_axis=0, tiled=True)
     weights = (w_in[0], w_qkv[0], w_proj[0], w_mid[0], w_up[0], w_down[0], w_out[0])
-    order = (lax.axis_index("pool") + jnp.arange(groups, dtype=jnp.int32)) % groups
-    done = refine_tiles(order[:1], outgoing, weights, columns)
-    chunks = refine_tiles(order[1:], landing, None, columns, done)
-    pieces = lax.all_to_all(chunks, ("pool", "dev"), split_axis=0, concat_axis=0, tiled=True)
-    where = jnp.stack([lax.axis_index("dev"), jnp.int32(columns)])
+    slot = lax.axis_index("near")
+    own = lax.axis_index("far") * 2 + slot
+    k = jnp.arange(8, dtype=jnp.int32)
+    place = jnp.where(
+        k < 4,
+        own ^ jnp.where(k == 0, 0, jnp.where(k == 3, 1, k + 1)),
+        jnp.where(k == 6, lax.axis_index("dev"), slot ^ (k & 1)),
+    )
+    near, ready = refine_tiles("refine_own", place, outgoing, 1, 0, 4, weights, columns)
+    far = refine_tiles("refine_far", place, landing, 2, 1, 4, None, columns, (near, False, ready))
+    far_pieces = lax.all_to_all(far, ("near", "dev"), split_axis=0, concat_axis=0, tiled=True)
+    near, _ = lax.optimization_barrier((near, far))
+    near = refine_tiles("refine_near", place, landing, 1, 3, 5, None, columns, (near, True, ready))
+    near_pieces = lax.all_to_all(near, ("near", "dev"), split_axis=0, concat_axis=0, tiled=True)
+    far_pieces = lax.ppermute(far_pieces, "far", [(0, 1), (1, 0)])
     return decode_band(
-        where, pieces, *flip_weights(dec_in, dec_mid), frames, groups, columns, side
+        place, 6, near_pieces, far_pieces, *flip_weights(dec_in, dec_mid), frames, columns, side
     )[None]
 
 
 def solution(mesh):
+    devices = mesh.devices
+    mesh = jax.sharding.Mesh(
+        devices.reshape(2, devices.shape[0] // 2, devices.shape[1]), (*POOL, "dev")
+    )
     in_specs = (
-        P("pool", None, None, "dev"),
-        P("pool", "dev", None, None),
-        P("pool", None, None, None, None),
-        P("pool", None, None),
-        P("pool", None, None),
-        P("pool", None, None, None, None),
-        P("pool", None, None),
-        P("pool", None, None),
-        P("pool", None, None, None, None),
+        P(POOL, None, None, "dev"),
+        P(POOL, "dev", None, None),
+        P(POOL, None, None, None, None),
+        P(POOL, None, None),
+        P(POOL, None, None),
+        P(POOL, None, None, None, None),
+        P(POOL, None, None),
+        P(POOL, None, None),
+        P(POOL, None, None, None, None),
         P(),
         P(),
     )
-    out_specs = P("pool", None, None, "dev", None)
+    out_specs = P(POOL, None, None, "dev", None)
     return jax.shard_map(shards, mesh=mesh, in_specs=in_specs, out_specs=out_specs, check_vma=False)

time: 110 us -> 108 us (0.982)
  waiting for transfers between devices: 19.9 us -> 8.94 us
  starting transfers between devices: 11.7 us -> 18.9 us
  Pallas kernels: 74.8 us -> 77.3 us
    all_to_all x2 -> x3, waiting for transfers between devices: 19.9 us -> 8.94 us  [the longest x1 8.57 us: shards(): lax.all_to_all(near, ('near', 'dev'), split_axis=0, concat_axis=0, tiled=...]
    all_to_all x2 -> x3, starting transfers between devices: 11.7 us -> 17.3 us  [the longest x1 6.5 us: shards(): lax.all_to_all(far, ('near', 'dev'), split_axis=0, concat_axis=0, tiled=T...]
    pallas_call x2 -> x3, Pallas kernels: 44.3 us -> 47.1 us  [refine_tiles(): pl.pallas_call(functools.partial(refine_kernel, side=side, bands=bands, f...]
    ppermute x0 -> x1, starting transfers between devices: none -> 1.52 us  [shards(): far_pieces = lax.ppermute(far_pieces, 'far', [(0, 1), (1, 0)])]
  transfers between devices with their start and end apart: 2 -> 4, of which waited for: 1 -> 2; matrix products, arithmetic and copies ran while one was open for 1% -> 1% of each run, Pallas kernels for 14% -> 26%
where the time goes in v3:
time: 108 us; the launch traced here: 107 us
  Pallas kernels  77.3 us (72%)
  starting transfers between devices  18.9 us (17%)
  waiting for transfers between devices  8.94 us (8%)
  local copies, waits for them, and re-layouts  1.72 us (2%)
    pallas_call x3, Pallas kernels, refine_tiles(): pl.pallas_call(functools.partial(refine_kernel, side=side, bands=bands, f...  47.1 us
    pallas_call x1, Pallas kernels, decode_band(): pl.pallas_call(functools.partial(decode_kernel, dev_at=dev_at, lanes_in_s...  25.8 us
    all_to_all x1, waiting for transfers between devices, shards(): lax.all_to_all(near, ('near', 'dev'), split_axis=0, concat_axis=0, tiled=...  8.57 us
    all_to_all x1, starting transfers between devices, shards(): lax.all_to_all(far, ('near', 'dev'), split_axis=0, concat_axis=0, tiled=T...  6.5 us
    all_to_all x1, starting transfers between devices, shards(): lax.all_to_all(near, ('near', 'dev'), split_axis=0, concat_axis=0, tiled=...  5.65 us
    all_to_all x1, starting transfers between devices, shards(): lax.all_to_all(outgoing, ('far', 'near'), split_axis=0, concat_axis=0, ti...  5.19 us
    pallas_call x1, Pallas kernels, flip_weights(): pl.pallas_call(flip_kernel, out_shape=[jax.ShapeDtypeStruct(w.shape[::-1]...  2.54 us
  transfers between devices with their start and end apart: 4, of which 2 were waited for; matrix products, arithmetic and copies ran while one was open for 1% of the time, Pallas kernels for 26%

profile of v3, /device:TPU:0, one launch (start us, length us, event | category | flops | bytes accessed | tf_op | source)
XLA Modules:
  0.0 107.4 jit_solution(17654237311960445722)
XLA Ops:
  0.0 1.9 %pick.1.refs_1_ = bf16[4,16,4224]{2,1,0:T(8,128)(2,1)} custom-call(s32[4]{0:T(128)} %bitcast.19, bf16[4,16,4096]{2,1,0:T(8,128)(2,1)} %bitcast.17), custom_call_target="tpu_custom_call" | custom-call | tf_op jit(solution)/shard_map/pick/pallas_call | solution.py:63
  1.9 5.2 %all-to-all-start = ((bf16[4,16,4224]{2,1,0:T(8,128)(2,1)}), bf16[4,16,4224]{2,1,0:T(8,128)(2,1)S(1)}, u32[]{:S(2)}, u32[]{:S(2)}) async-start(bf16[4,16,4224]{2,1,0:T(8,128)(2,1)} %pick.1.refs_1_), calls=%async_computation | async-start | bytes 1081344 | tf_op jit(solution)/shard_map/all_to_all | solution.py:475
  7.1 0.5 compare_select_fusion.3.refs_0_.place_ref
  7.6 12.7 %refine_own.1 = (bf16[16,104,128]{2,1,0:T(8,128)(2,1)}, bf16[128,144]{1,0:T(8,128)(2,1)}, bf16[384,128]{1,0:T(8,128)(2,1)}, bf16[128,128]{1,0:T(8,128)(2,1)}, bf...) custom-call(s32[8]{0:T(128)} %compare_select_fusion.3.refs_0_.place_ref, ...), custom_call_target="tpu_custom_call" | custom-call | flops 4000000000 | bytes 2097152 | tf_op jit(solution)/shard_map/refine_own/pallas_call | solution.py:284
  20.4 0.0 all-to-all-done.refs_1_
  20.4 0.0 copy-start.1
  20.4 0.8 copy-done.1
  21.2 22.1 %refine_far.1 = bf16[16,104,128]{2,1,0:T(8,128)(2,1)} custom-call(s32[8]{0:T(128)} %compare_select_fusion.3.refs_0_.place_ref, bf16[4,16,4224]{2,1,0:T(8,128)(2,1)} %copy-done.1, bf16[16,104,128]{2,1,0:T(8,128)(2,1)} %get-tuple-element.24.refs_2_, bf16[144,128]{1,0:T(8,128)(2,1)} %bitcast.26, bf16[128,144]{1,0:T(8,128)(2,1)} %get-tuple-element.17.refs_4_, ...), custom_call_target="tpu_custom_call" | custom-call | flops 8000000000 | bytes 4194304 | tf_op jit(solution)/shard_map/refine_far/pallas_call | solution.py:284
  43.2 6.5 %all-to-all-start.2 = ((bf16[16,104,128]{2,1,0:T(8,128)(2,1)}), bf16[16,104,128]{2,1,0:T(8,128)(2,1)S(1)}, u32[]{:S(2)}, u32[]{:S(2)}) async-start(bf16[16,104,128]{2,1,0:T(8,128)(2,1)} %refine_far.1), calls=%async_computation.2 | async-start | bytes 851968 | tf_op jit(solution)/shard_map/all_to_all | solution.py:487
  49.8 12.3 %refine_near.1 = bf16[16,104,128]{2,1,0:T(8,128)(2,1)} custom-call(s32[8]{0:T(128)} %compare_select_fusion.3.refs_0_.place_ref, bf16[4,16,4224]{2,1,0:T(8,128)(2,1)} %copy-done.1, bf16[16,104,128]{2,1,0:T(8,128)(2,1)} %get-tuple-element.24.refs_2_, bf16[144,128]{1,0:T(8,128)(2,1)} %bitcast.27, ...), custom_call_target="tpu_custom_call", output_to_operand_aliasing={{}: (2, {})} | custom-call | flops 4000000000 | bytes 2097152 | tf_op jit(solution)/shard_map/refine_near/pallas_call | solution.py:284
  62.0 0.4 all-to-all-done.2
  62.4 5.6 %all-to-all-start.1 = ((bf16[16,104,128]{2,1,0:T(8,128)(2,1)}), bf16[16,104,128]{2,1,0:T(8,128)(2,1)S(1)}, u32[]{:S(2)}, u32[]{:S(2)}) async-start(bf16[16,104,128]{2,1,0:T(8,128)(2,1)} %refine_near.1), calls=%async_computation.1 | async-start | bytes 851968 | tf_op jit(solution)/shard_map/all_to_all | solution.py:490
  68.1 1.5 %collective-permute-start = (bf16[16,104,128]{2,1,0:T(8,128)(2,1)S(1)}, bf16[16,104,128]{2,1,0:T(8,128)(2,1)S(1)}, u32[]{:S(2)}, u32[]{:S(2)}) collective-permute-start(bf16[16,104,128]{2,1,0:T(8,128)(2,1)S(1)} %all-to-all-done.2), channel_id=1, source_target_pairs={{0,16},{16,0},{1,17},{17,1},{2,18},{18,2},{3,19},{19,3},{4,20},{20... | collective-permute-start | bytes 1277960 | tf_op jit(solution)/shard_map/ppermute | solution.py:491
  69.6 2.5 %flip.1 = (bf16[192,432]{1,0:T(8,128)(2,1)}, bf16[192,1728]{1,0:T(8,128)(2,1)}) custom-call(bf16[432,192]{1,0:T(8,128)(2,1)} %bitcast.18, bf16[1728,192]{1,0:T(8,128)(2,1)} %bitcast.16), custom_call_target="tpu_custom_call" | custom-call | flops 1000000 | bytes 2097152 | tf_op jit(solution)/shard_map/flip/pallas_call | solution.py:430
  72.1 8.6 %all-to-all-done.1.near_ref = bf16[16,104,128]{2,1,0:T(8,128)(2,1)S(1)} async-done(((bf16[16,104,128]{2,1,0:T(8,128)(2,1)}), bf16[16,104,128]{2,1,0:T(8,128)(2,1)S(1)}, u32[]{:S(2)}, u32[]{:S(2)}) %all-to-all-start.1) | async-done | bytes 426016 | tf_op jit(solution)/shard_map/all_to_all | solution.py:490
  80.7 0.0 copy-start
  80.7 0.0 collective-permute-done.far_ref
  80.7 0.0 copy-start.2
  80.7 0.8 copy-done
  81.5 0.2 copy-done.2
  81.6 25.8 %decode.1 = bf16[4,192,8,512]{3,2,1,0:T(8,128)(2,1)} custom-call(s32[8]{0:T(128)} %compare_select_fusion.3.refs_0_.place_ref, bf16[16,104,128]{2,1,0:T(8,128)(2,1)} %copy-done, bf16[16,104,128]{2,1,0:T(8,128)(2,1)} %copy-done.2, bf16[192,432]{1,0:T(8,128)(2,1)} %get-tuple-element.25.t_in, bf16[192,1728]{1,0:T(8,128)(2,1)} %get-tuple-element.26.t_mid), custom_call_target="tpu_custom_call" | custom-call | tf_op jit(solution)/shard_map/decode/pallas_call | solution.py:447
Async XLA Ops:
  1.9 18.5 %all-to-all-start = ((bf16[4,16,4224]{2,1,0:T(8,128)(2,1)}), bf16[4,16,4224]{2,1,0:T(8,128)(2,1)S(1)}, u32[]{:S(2)}, u32[]{:S(2)}) async-start(bf16[4,16,4224]{2,1,0:T(8,128)(2,1)} %pick.1.refs_1_), calls=%async_computation | async-start | bytes 1081344 | tf_op jit(solution)/shard_map/all_to_all | solution.py:475
  20.4 0.8 copy-start.1
  43.2 19.2 %all-to-all-start.2 = ((bf16[16,104,128]{2,1,0:T(8,128)(2,1)}), bf16[16,104,128]{2,1,0:T(8,128)(2,1)S(1)}, u32[]{:S(2)}, u32[]{:S(2)}) async-start(bf16[16,104,128]{2,1,0:T(8,128)(2,1)} %refine_far.1), calls=%async_computation.2 | async-start | bytes 851968 | tf_op jit(solution)/shard_map/all_to_all | solution.py:487
  62.4 18.3 %all-to-all-start.1 = ((bf16[16,104,128]{2,1,0:T(8,128)(2,1)}), bf16[16,104,128]{2,1,0:T(8,128)(2,1)S(1)}, u32[]{:S(2)}, u32[]{:S(2)}) async-start(bf16[16,104,128]{2,1,0:T(8,128)(2,1)} %refine_near.1), calls=%async_computation.1 | async-start | bytes 851968 | tf_op jit(solution)/shard_map/all_to_all | solution.py:490
  68.1 12.6 %collective-permute-start = (bf16[16,104,128]{2,1,0:T(8,128)(2,1)S(1)}, bf16[16,104,128]{2,1,0:T(8,128)(2,1)S(1)}, u32[]{:S(2)}, u32[]{:S(2)}) collective-permute-start(bf16[16,104,128]{2,1,0:T(8,128)(2,1)S(1)} %all-to-all-done.2), channel_id=1, source_target_pairs={{0,16},{16,0},{1,17},{17,1},{2,18},{18,2},{3,19},{19,3},{4,20},{20... | collective-permute-start | bytes 1277960 | tf_op jit(solution)/shard_map/ppermute | solution.py:491
  80.7 0.8 copy-start
  80.7 0.9 copy-start.2

commit v4 on v3

--- a/solution.py
+++ b/solution.py
@@ -27,8 +27,7 @@
     return lax.dot_general(a, b, (((0,), (0,)), ((), ())), preferred_element_type=F32)
 
 
-def silu(x):
-    half = 0.5 * x
+def silu_twice(half):
     return half + half * jnp.tanh(half)
 
 
@@ -90,11 +89,11 @@
     assert side == WIN * WIN and pair == 2 and 2 * side == LANES
 
     if first:
-        for flipped, weight in (
-            (t_in, w_in), (t_qkv, w_qkv), (t_proj, w_proj),
-            (t_mid, w_mid), (t_up, w_up), (t_down, w_down),
+        for flipped, weight, factor in (
+            (t_in, w_in, 1.0), (t_qkv, w_qkv, 1.0), (t_proj, w_proj, 1.0),
+            (t_mid, w_mid, 0.5), (t_up, w_up, 0.5), (t_down, w_down, 1.0),
         ):
-            flipped[...] = weight[...].astype(F32).T.astype(BF16)
+            flipped[...] = (weight[...].astype(F32) * factor).T.astype(BF16)
         src = lax.broadcasted_iota(jnp.int32, (chunk, chunk), 0)
         dst = lax.broadcasted_iota(jnp.int32, (chunk, chunk), 1)
         want = ((dst >> 3) & 7) * side + (dst >> 6) * WIN + (dst & 7)
@@ -212,12 +211,12 @@
         around = jnp.concatenate(
             [odd[:, pl.ds(base, chunk)], even[:, after], odd[:, after]], axis=0
         )
-        convolved = att[:, pl.ds(base, chunk)] + silu(dot(t_mid[...], around))
+        convolved = att[:, pl.ds(base, chunk)] + silu_twice(dot(t_mid[...], around))
         att[:, pl.ds(base, chunk)] = convolved
         mixed_ref[:, pl.ds(base, chunk)] = norm_channels(convolved).astype(BF16)
 
     def finish2(base):
-        wide[:, pl.ds(base, chunk)] = silu(dot(t_up[...], mixed_ref[:, pl.ds(base, chunk)])).astype(BF16)
+        wide[:, pl.ds(base, chunk)] = silu_twice(dot(t_up[...], mixed_ref[:, pl.ds(base, chunk)])).astype(BF16)
 
     def finish3(base):
         finished = att[:, pl.ds(base, chunk)] + dot(t_down[...], wide[:, pl.ds(base, chunk)])
@@ -314,7 +313,7 @@
 
 
 def decode_kernel(
-    place_ref, near_ref, far_ref, t_in, t_mid, out_ref, strip, act, rows_out,
+    place_ref, near_ref, far_ref, t_in, t_a, t_b, t_c, t_e, out_ref, strip, act, rows_out, waves,
     *, dev_at, lanes_in_strip, side,
 ):
     frames, _, _, cols = strip.shape
@@ -383,7 +382,7 @@
             ],
             axis=0,
         )
-        value = silu(dot(t_in[...], around))
+        value = silu_twice(dot(t_in[...], around))
         if y == 0:
             value = jnp.where(first_row, 0.0, value)
         if y == band + 1:
@@ -399,49 +398,85 @@
             col < cols - 1, pltpu.roll(value, cols - 1, 1), 0
         )
 
-    def out_row(y):
-        top = y * 3 * dec
-        value = dot(t_mid[...], act[top : top + 9 * dec, :])
-        value = value + act[top + 4 * dec : top + 5 * dec, :].astype(F32)
-        for k in range(cols // LANES):
-            rows_out[pl.ds(k * dec * band + y, dec, stride=band), :] = value[
-                :, k * LANES : (k + 1) * LANES
+    lead = t_b.shape[1]
+
+    def mix_pair(y):
+        r = [act[(y + k) * 3 * dec : (y + k) * 3 * dec + lead, :] for k in range(4)]
+        top = y * 2 * lead
+        for k, wave in enumerate((r[0] - r[2], r[1] + r[2], r[2] - r[1], r[1] - r[3])):
+            waves[top + k * lead : top + (k + 1) * lead, :] = wave
+
+    def out_pair(y):
+        def wave(k):
+            top = y * 2 * lead + k * lead
+            return waves[top : top + lead, :]
+
+        def rest(row):
+            return [
+                act[(row + dy) * 3 * dec + lead : (row + dy + 1) * 3 * dec, :] for dy in range(3)
             ]
+
+        first = dot(t_a[...], jnp.concatenate([wave(0)] + rest(y), axis=0))
+        even_part = dot(t_b[...], wave(1))
+        odd_part = dot(t_c[...], wave(2))
+        last = dot(t_e[...], jnp.concatenate([wave(3)] + rest(y + 1), axis=0))
+        for row, value in ((y, first + (even_part + odd_part)), (y + 1, last + (even_part - odd_part))):
+            top = row * 3 * dec
+            value = value + act[top + 4 * dec : top + 5 * dec, :].astype(F32)
+            for k in range(cols // LANES):
+                rows_out[pl.ds(k * dec * band + row, dec, stride=band), :] = value[
+                    :, k * LANES : (k + 1) * LANES
+                ]
 
     for y in range(band + 2):
         act_row(y)
     for y in range(band + 2):
         side_rows(y)
-    for y in range(band):
-        out_row(y)
+    for y in range(0, band, 2):
+        mix_pair(y)
+    for y in range(0, band, 2):
+        out_pair(y)
     for k in range(cols // LANES):
         done = rows_out[k * dec * band : (k + 1) * dec * band, :]
         out_ref[0, :, :, k * LANES : (k + 1) * LANES] = done.reshape(dec, band, LANES).astype(BF16)
 
 
-def flip_kernel(w_in, w_mid, t_in, t_mid):
-    t_in[...] = w_in[...].astype(F32).T.astype(BF16)
-    t_mid[...] = w_mid[...].astype(F32).T.astype(BF16)
+def flip_kernel(w_in, w_mid, t_in, t_a, t_b, t_c, t_e):
+    t_in[...] = (w_in[...].astype(F32) * 0.5).T.astype(BF16)
+    depth = w_mid.shape[0] // 3
+    lead = t_b.shape[1]
+    g = [w_mid[k * depth : k * depth + lead, :].astype(F32) for k in range(3)]
+    rest = [w_mid[k * depth + lead : (k + 1) * depth, :].astype(F32) for k in range(3)]
+    t_a[...] = jnp.concatenate([g[0]] + rest, axis=0).T.astype(BF16)
+    t_b[...] = (0.5 * (g[0] + g[1] + g[2])).T.astype(BF16)
+    t_c[...] = (0.5 * (g[0] - g[1] + g[2])).T.astype(BF16)
+    t_e[...] = jnp.concatenate([-g[2]] + rest, axis=0).T.astype(BF16)
 
 
 def flip_weights(dec_in, dec_mid):
     dec = dec_in.shape[-1]
     both = (dec_in.reshape(-1, dec), dec_mid.reshape(-1, dec))
+    depth = both[1].shape[0] // 3
+    lead = depth // 256 * 256
+    full = 3 * depth - 2 * lead
+    shapes = [(dec, n) for n in (both[0].shape[0], full, lead, lead, full)]
     return pl.pallas_call(
         flip_kernel,
-        out_shape=[jax.ShapeDtypeStruct(w.shape[::-1], BF16) for w in both],
+        out_shape=[jax.ShapeDtypeStruct(shape, BF16) for shape in shapes],
         in_specs=[pl.BlockSpec(memory_space=pltpu.VMEM)] * 2,
-        out_specs=[pl.BlockSpec(memory_space=pltpu.VMEM)] * 2,
+        out_specs=[pl.BlockSpec(memory_space=pltpu.VMEM)] * len(shapes),
         cost_estimate=pl.CostEstimate(flops=10**6, bytes_accessed=2**21, transcendentals=0),
         name="flip",
     )(*both)
 
 
-def decode_band(place, dev_at, near, far, t_in, t_mid, frames, columns, side):
-    dec = t_in.shape[0]
-    ch = t_in.shape[1] // 27
+def decode_band(place, dev_at, near, far, flipped, frames, columns, side):
+    dec = flipped[0].shape[0]
+    ch = flipped[0].shape[1] // 27
+    lead = flipped[2].shape[1]
     rows = near.shape[1]
     band = (rows - META) // ch * LANES // side - 4
+    assert band % 2 == 0
     cols = columns * side
     whole = pl.BlockSpec(memory_space=pltpu.VMEM)
     return pl.pallas_call(
@@ -450,17 +485,18 @@
         grid_spec=pltpu.PrefetchScalarGridSpec(
             num_scalar_prefetch=1,
             grid=(frames,),
-            in_specs=[whole] * 4,
+            in_specs=[whole] * (2 + len(flipped)),
             out_specs=pl.BlockSpec((1, dec, band, cols), lambda f, w: (f, 0, 0, 0)),
             scratch_shapes=[
                 pltpu.VMEM((frames + 2, band + 4, 3 * ch, cols), BF16),
                 pltpu.VMEM(((band + 2) * 3 * dec, cols), BF16),
                 pltpu.VMEM((cols // LANES * dec * band, LANES), F32),
+                pltpu.VMEM((band * 2 * lead, cols), BF16),
             ],
         ),
         compiler_params=pltpu.CompilerParams(vmem_limit_bytes=VMEM_LIMIT),
         name="decode",
-    )(place, near, far, t_in, t_mid)
+    )(place, near, far, *flipped)
 
 
 def shards(latent, tile_routes, w_in, w_qkv, w_proj, w_mid, w_up, w_down, w_out, dec_in, dec_mid):
@@ -490,7 +526,7 @@
     near_pieces = lax.all_to_all(near, ("near", "dev"), split_axis=0, concat_axis=0, tiled=True)
     far_pieces = lax.ppermute(far_pieces, "far", [(0, 1), (1, 0)])
     return decode_band(
-        place, 6, near_pieces, far_pieces, *flip_weights(dec_in, dec_mid), frames, columns, side
+        place, 6, near_pieces, far_pieces, flip_weights(dec_in, dec_mid), frames, columns, side
     )[None]
 
 

time: 108 us -> 103 us (0.954)
  Pallas kernels: 77.3 us -> 72.4 us
    pallas_call x1, Pallas kernels: 25.8 us -> 23 us  [decode_band(): pl.pallas_call(functools.partial(decode_kernel, dev_at=dev_at, lanes_in_s...]
    pallas_call x3, Pallas kernels: 47.1 us -> 44.7 us  [refine_tiles(): pl.pallas_call(functools.partial(refine_kernel, side=side, bands=bands, f...]
where the time goes in v4:
time: 103 us; the launch traced here: 102 us
  Pallas kernels  72.4 us (70%)
  starting transfers between devices  18.2 us (18%)
  waiting for transfers between devices  9.37 us (9%)
  local copies, waits for them, and re-layouts  1.72 us (2%)
    pallas_call x3, Pallas kernels, refine_tiles(): pl.pallas_call(functools.partial(refine_kernel, side=side, bands=bands, f...  44.7 us
    pallas_call x1, Pallas kernels, decode_band(): pl.pallas_call(functools.partial(decode_kernel, dev_at=dev_at, lanes_in_s...  23 us
    all_to_all x1, waiting for transfers between devices, shards(): lax.all_to_all(near, ('near', 'dev'), split_axis=0, concat_axis=0, tiled=...  8.41 us
    all_to_all x1, starting transfers between devices, shards(): lax.all_to_all(far, ('near', 'dev'), split_axis=0, concat_axis=0, tiled=T...  6.42 us
    all_to_all x1, starting transfers between devices, shards(): lax.all_to_all(outgoing, ('far', 'near'), split_axis=0, concat_axis=0, ti...  5.19 us
    all_to_all x1, starting transfers between devices, shards(): lax.all_to_all(near, ('near', 'dev'), split_axis=0, concat_axis=0, tiled=...  5.04 us
    pallas_call x1, Pallas kernels, flip_weights(): pl.pallas_call(flip_kernel, out_shape=[jax.ShapeDtypeStruct(shape, BF16)...  2.71 us
  transfers between devices with their start and end apart: 4, of which 2 were waited for; matrix products, arithmetic and copies ran while one was open for 1% of the time, Pallas kernels for 26%

profile of v4, /device:TPU:0, one launch (start us, length us, event | category | flops | bytes accessed | tf_op | source)
XLA Modules:
  0.0 102.2 jit_solution(17204291898489667211)
XLA Ops:
  0.0 1.9 %pick.1.refs_1_ = bf16[4,16,4224]{2,1,0:T(8,128)(2,1)} custom-call(s32[4]{0:T(128)} %bitcast.19, bf16[4,16,4096]{2,1,0:T(8,128)(2,1)} %bitcast.17), custom_call_target="tpu_custom_call" | custom-call | tf_op jit(solution)/shard_map/pick/pallas_call | solution.py:62
  1.9 5.2 %all-to-all-start = ((bf16[4,16,4224]{2,1,0:T(8,128)(2,1)}), bf16[4,16,4224]{2,1,0:T(8,128)(2,1)S(1)}, u32[]{:S(2)}, u32[]{:S(2)}) async-start(bf16[4,16,4224]{2,1,0:T(8,128)(2,1)} %pick.1.refs_1_), calls=%async_computation | async-start | bytes 1081344 | tf_op jit(solution)/shard_map/all_to_all | solution.py:511
  7.1 0.5 compare_select_fusion.3.refs_0_.place_ref
  7.6 12.1 %refine_own.1 = (bf16[16,104,128]{2,1,0:T(8,128)(2,1)}, bf16[128,144]{1,0:T(8,128)(2,1)}, bf16[384,128]{1,0:T(8,128)(2,1)}, bf16[128,128]{1,0:T(8,128)(2,1)}, bf...) custom-call(s32[8]{0:T(128)} %compare_select_fusion.3.refs_0_.place_ref, ...), custom_call_target="tpu_custom_call" | custom-call | flops 4000000000 | bytes 2097152 | tf_op jit(solution)/shard_map/refine_own/pallas_call | solution.py:283
  19.8 0.0 all-to-all-done.refs_1_
  19.8 0.0 copy-start.1
  19.8 0.8 copy-done.1
  20.6 20.9 %refine_far.1 = bf16[16,104,128]{2,1,0:T(8,128)(2,1)} custom-call(s32[8]{0:T(128)} %compare_select_fusion.3.refs_0_.place_ref, bf16[4,16,4224]{2,1,0:T(8,128)(2,1)} %copy-done.1, bf16[16,104,128]{2,1,0:T(8,128)(2,1)} %get-tuple-element.27.refs_2_, bf16[144,128]{1,0:T(8,128)(2,1)} %bitcast.26, bf16[128,144]{1,0:T(8,128)(2,1)} %get-tuple-element.20.refs_4_, ...), custom_call_target="tpu_custom_call" | custom-call | flops 8000000000 | bytes 4194304 | tf_op jit(solution)/shard_map/refine_far/pallas_call | solution.py:283
  41.5 6.4 %all-to-all-start.2 = ((bf16[16,104,128]{2,1,0:T(8,128)(2,1)}), bf16[16,104,128]{2,1,0:T(8,128)(2,1)S(1)}, u32[]{:S(2)}, u32[]{:S(2)}) async-start(bf16[16,104,128]{2,1,0:T(8,128)(2,1)} %refine_far.1), calls=%async_computation.2 | async-start | bytes 851968 | tf_op jit(solution)/shard_map/all_to_all | solution.py:523
  47.9 11.7 %refine_near.1 = bf16[16,104,128]{2,1,0:T(8,128)(2,1)} custom-call(s32[8]{0:T(128)} %compare_select_fusion.3.refs_0_.place_ref, bf16[4,16,4224]{2,1,0:T(8,128)(2,1)} %copy-done.1, bf16[16,104,128]{2,1,0:T(8,128)(2,1)} %get-tuple-element.27.refs_2_, bf16[144,128]{1,0:T(8,128)(2,1)} %bitcast.27, ...), custom_call_target="tpu_custom_call", output_to_operand_aliasing={{}: (2, {})} | custom-call | flops 4000000000 | bytes 2097152 | tf_op jit(solution)/shard_map/refine_near/pallas_call | solution.py:283
  59.6 1.0 all-to-all-done.2
  60.6 5.0 %all-to-all-start.1 = ((bf16[16,104,128]{2,1,0:T(8,128)(2,1)}), bf16[16,104,128]{2,1,0:T(8,128)(2,1)S(1)}, u32[]{:S(2)}, u32[]{:S(2)}) async-start(bf16[16,104,128]{2,1,0:T(8,128)(2,1)} %refine_near.1), calls=%async_computation.1 | async-start | bytes 851968 | tf_op jit(solution)/shard_map/all_to_all | solution.py:526
  65.6 1.5 %collective-permute-start = (bf16[16,104,128]{2,1,0:T(8,128)(2,1)S(1)}, bf16[16,104,128]{2,1,0:T(8,128)(2,1)S(1)}, u32[]{:S(2)}, u32[]{:S(2)}) collective-permute-start(bf16[16,104,128]{2,1,0:T(8,128)(2,1)S(1)} %all-to-all-done.2), channel_id=1, source_target_pairs={{0,16},{16,0},{1,17},{17,1},{2,18},{18,2},{3,19},{19,3},{4,20},{20... | collective-permute-start | bytes 1277960 | tf_op jit(solution)/shard_map/ppermute | solution.py:527
  67.2 2.7 %flip.1 = (bf16[192,432]{1,0:T(8,128)(2,1)}, bf16[192,704]{1,0:T(8,128)(2,1)}, bf16[192,512]{1,0:T(8,128)(2,1)}, bf16[192,512]{1,0:T(8,128)(2,1)}, bf16[192,704]{1,0:T(8,128)(2,1)}) custom-call(bf16[432,192]{1,0:T(8,128)(2,1)} %bitcast.18, bf16[1728,192]{1,0:T(8,128)(2,1)} %bitcast.16), custom_call_target="tpu_custom_call" | custom-call | flops 1000000 | bytes 2097152 | tf_op jit(solution)/shard_map/flip/pallas_call | solution.py:463
  69.9 8.4 %all-to-all-done.1.near_ref = bf16[16,104,128]{2,1,0:T(8,128)(2,1)S(1)} async-done(((bf16[16,104,128]{2,1,0:T(8,128)(2,1)}), bf16[16,104,128]{2,1,0:T(8,128)(2,1)S(1)}, u32[]{:S(2)}, u32[]{:S(2)}) %all-to-all-start.1) | async-done | bytes 426016 | tf_op jit(solution)/shard_map/all_to_all | solution.py:526
  78.3 0.0 copy-start
  78.3 0.0 collective-permute-done.far_ref
  78.3 0.0 copy-start.2
  78.3 0.7 copy-done
  79.0 0.2 copy-done.2
  79.2 23.0 %decode.1 = bf16[4,192,8,512]{3,2,1,0:T(8,128)(2,1)} custom-call(s32[8]{0:T(128)} %compare_select_fusion.3.refs_0_.place_ref, bf16[16,104,128]{2,1,0:T(8,128)(2,1)} %copy-done, bf16[16,104,128]{2,1,0:T(8,128)(2,1)} %copy-done.2, bf16[192,432]{1,0:T(8,128)(2,1)} %get-tuple-element.28.t_in, bf16[192,704]{1,0:T(8,128)(2,1)} %get-tuple-element.29.t_a, ...), custom_call_target="tpu_custom_call" | custom-call | tf_op jit(solution)/shard_map/decode/pallas_call | solution.py:482
Async XLA Ops:
  1.9 17.9 %all-to-all-start = ((bf16[4,16,4224]{2,1,0:T(8,128)(2,1)}), bf16[4,16,4224]{2,1,0:T(8,128)(2,1)S(1)}, u32[]{:S(2)}, u32[]{:S(2)}) async-start(bf16[4,16,4224]{2,1,0:T(8,128)(2,1)} %pick.1.refs_1_), calls=%async_computation | async-start | bytes 1081344 | tf_op jit(solution)/shard_map/all_to_all | solution.py:511
  19.8 0.8 copy-start.1
  41.5 19.1 %all-to-all-start.2 = ((bf16[16,104,128]{2,1,0:T(8,128)(2,1)}), bf16[16,104,128]{2,1,0:T(8,128)(2,1)S(1)}, u32[]{:S(2)}, u32[]{:S(2)}) async-start(bf16[16,104,128]{2,1,0:T(8,128)(2,1)} %refine_far.1), calls=%async_computation.2 | async-start | bytes 851968 | tf_op jit(solution)/shard_map/all_to_all | solution.py:523
  60.6 17.7 %all-to-all-start.1 = ((bf16[16,104,128]{2,1,0:T(8,128)(2,1)}), bf16[16,104,128]{2,1,0:T(8,128)(2,1)S(1)}, u32[]{:S(2)}, u32[]{:S(2)}) async-start(bf16[16,104,128]{2,1,0:T(8,128)(2,1)} %refine_near.1), calls=%async_computation.1 | async-start | bytes 851968 | tf_op jit(solution)/shard_map/all_to_all | solution.py:526
  65.6 12.6 %collective-permute-start = (bf16[16,104,128]{2,1,0:T(8,128)(2,1)S(1)}, bf16[16,104,128]{2,1,0:T(8,128)(2,1)S(1)}, u32[]{:S(2)}, u32[]{:S(2)}) collective-permute-start(bf16[16,104,128]{2,1,0:T(8,128)(2,1)S(1)} %all-to-all-done.2), channel_id=1, source_target_pairs={{0,16},{16,0},{1,17},{17,1},{2,18},{18,2},{3,19},{19,3},{4,20},{20... | collective-permute-start | bytes 1277960 | tf_op jit(solution)/shard_map/ppermute | solution.py:527
  78.3 0.8 copy-start
  78.3 0.9 copy-start.2

commit v5 on v4

--- a/solution.py
+++ b/solution.py
@@ -313,11 +313,10 @@
 
 
 def decode_kernel(
-    place_ref, near_ref, far_ref, t_in, t_a, t_b, t_c, t_e, out_ref, strip, act, rows_out, waves,
+    place_ref, near_ref, far_ref, t_in, t_a, t_b, t_c, t_e, out_ref, strip, act, rows_out, waves, ahead,
     *, dev_at, lanes_in_strip, side,
 ):
-    frames, _, _, cols = strip.shape
-    frames -= 2
+    cols = strip.shape[3]
     frame = pl.program_id(0)
     band = out_ref.shape[2]
     dec = out_ref.shape[1]
@@ -334,41 +333,47 @@
     low = lane < side
     col = lane_iota(cols)
 
+    def build(f, into):
+        note_at = tall * side // LANES * ch
+        picks = [
+            [
+                jnp.where(
+                    sets[g][d][note_at : note_at + 1, :].astype(F32).astype(jnp.int32) == f, 1.0, 0.0
+                )
+                for d in range(columns)
+            ]
+            for g in range(groups)
+        ]
+        for j in range(tall // 2):
+            both = [
+                sum(
+                    sets[g][d][j * ch : (j + 1) * ch, :].astype(F32) * picks[g][d]
+                    for g in range(groups)
+                )
+                for d in range(columns)
+            ]
+            turned = [pltpu.roll(x, side, 1) for x in both]
+            first = [jnp.where(low, both[d], turned[d + 1]) for d in range(0, columns, 2)]
+            second = [jnp.where(low, turned[d], both[d + 1]) for d in range(0, columns, 2)]
+            for y, parts in ((2 * j, first), (2 * j + 1, second)):
+                line = jnp.concatenate(parts, axis=1)
+                left = jnp.where(col > 0, pltpu.roll(line, 1, 1), 0.0)
+                right = jnp.where(col < cols - 1, pltpu.roll(line, cols - 1, 1), 0.0)
+                whole = jnp.concatenate([left, line, right], axis=0).astype(BF16)
+                into(y, whole)
+
     @pl.when(frame == 0)
     def _():
         strip[0:2] = jnp.zeros((2,) + strip.shape[1:], BF16)
-        note_at = tall * side // LANES * ch
-        notes = [
-            [sets[g][d][note_at : note_at + 1, :].astype(F32) for d in range(columns)]
-            for g in range(groups)
-        ]
-        for f in range(frames):
-            picks = [
-                [jnp.where(notes[g][d] == f, 1.0, 0.0) for d in range(columns)]
-                for g in range(groups)
-            ]
-            for j in range(tall // 2):
-                both = []
-                for d in range(columns):
-                    both.append(
-                        sum(
-                            sets[g][d][j * ch : (j + 1) * ch, :].astype(F32)
-                            * picks[g][d]
-                            for g in range(groups)
-                        )
-                    )
-                turned = [pltpu.roll(x, side, 1) for x in both]
-                first = [
-                    jnp.where(low, both[d], turned[d + 1]) for d in range(0, columns, 2)
-                ]
-                second = [
-                    jnp.where(low, turned[d], both[d + 1]) for d in range(0, columns, 2)
-                ]
-                for y, parts in ((2 * j, first), (2 * j + 1, second)):
-                    line = jnp.concatenate(parts, axis=1)
-                    left = jnp.where(col > 0, pltpu.roll(line, 1, 1), 0.0)
-                    right = jnp.where(col < cols - 1, pltpu.roll(line, cols - 1, 1), 0.0)
-                    strip[f + 2, y] = jnp.concatenate([left, line, right], axis=0).astype(BF16)
+
+        def here(y, rows):
+            strip[2, y] = rows
+
+        build(frame, here)
+
+    @pl.when(frame > 0)
+    def _():
+        strip[pl.ds(frame + 2, 1)] = ahead[...][None]
 
     first_row = place_ref[dev_at] == 0
     last_row = place_ref[dev_at] == cols // side - 1
@@ -430,6 +435,10 @@
 
     for y in range(band + 2):
         act_row(y)
+    def there(y, rows):
+        ahead[y] = rows
+
+    build(frame + 1, there)
     for y in range(band + 2):
         side_rows(y)
     for y in range(0, band, 2):
@@ -492,6 +501,7 @@
                 pltpu.VMEM(((band + 2) * 3 * dec, cols), BF16),
                 pltpu.VMEM((cols // LANES * dec * band, LANES), F32),
                 pltpu.VMEM((band * 2 * lead, cols), BF16),
+                pltpu.VMEM((band + 4, 3 * ch, cols), BF16),
             ],
         ),
         compiler_params=pltpu.CompilerParams(vmem_limit_bytes=VMEM_LIMIT),

time: 103 us -> 102 us (level)
  no operation moved by 1% of the time
where the time goes in v5:
time: 102 us; the launch traced here: 101 us
  Pallas kernels  71.4 us (70%)
  starting transfers between devices  18.2 us (18%)
  waiting for transfers between devices  9.37 us (9%)
  local copies, waits for them, and re-layouts  1.72 us (2%)
    pallas_call x3, Pallas kernels, refine_tiles(): pl.pallas_call(functools.partial(refine_kernel, side=side, bands=bands, f...  44.7 us
    pallas_call x1, Pallas kernels, decode_band(): pl.pallas_call(functools.partial(decode_kernel, dev_at=dev_at, lanes_in_s...  22 us
    all_to_all x1, waiting for transfers between devices, shards(): lax.all_to_all(near, ('near', 'dev'), split_axis=0, concat_axis=0, tiled=...  8.41 us
    all_to_all x1, starting transfers between devices, shards(): lax.all_to_all(far, ('near', 'dev'), split_axis=0, concat_axis=0, tiled=T...  6.42 us
    all_to_all x1, starting transfers between devices, shards(): lax.all_to_all(outgoing, ('far', 'near'), split_axis=0, concat_axis=0, ti...  5.19 us
    all_to_all x1, starting transfers between devices, shards(): lax.all_to_all(near, ('near', 'dev'), split_axis=0, concat_axis=0, tiled=...  5.04 us
    pallas_call x1, Pallas kernels, flip_weights(): pl.pallas_call(flip_kernel, out_shape=[jax.ShapeDtypeStruct(shape, BF16)...  2.71 us
  transfers between devices with their start and end apart: 4, of which 2 were waited for; matrix products, arithmetic and copies ran while one was open for 1% of the time, Pallas kernels for 26%

profile of v5, /device:TPU:0, one launch (start us, length us, event | category | flops | bytes accessed | tf_op | source)
XLA Modules:
  0.0 101.2 jit_solution(3318221181620013074)
XLA Ops:
  0.0 1.9 %pick.1.refs_1_ = bf16[4,16,4224]{2,1,0:T(8,128)(2,1)} custom-call(s32[4]{0:T(128)} %bitcast.19, bf16[4,16,4096]{2,1,0:T(8,128)(2,1)} %bitcast.17), custom_call_target="tpu_custom_call" | custom-call | tf_op jit(solution)/shard_map/pick/pallas_call | solution.py:62
  1.9 5.2 %all-to-all-start = ((bf16[4,16,4224]{2,1,0:T(8,128)(2,1)}), bf16[4,16,4224]{2,1,0:T(8,128)(2,1)S(1)}, u32[]{:S(2)}, u32[]{:S(2)}) async-start(bf16[4,16,4224]{2,1,0:T(8,128)(2,1)} %pick.1.refs_1_), calls=%async_computation | async-start | bytes 1081344 | tf_op jit(solution)/shard_map/all_to_all | solution.py:521
  7.1 0.5 compare_select_fusion.3.refs_0_.place_ref
  7.6 12.1 %refine_own.1 = (bf16[16,104,128]{2,1,0:T(8,128)(2,1)}, bf16[128,144]{1,0:T(8,128)(2,1)}, bf16[384,128]{1,0:T(8,128)(2,1)}, bf16[128,128]{1,0:T(8,128)(2,1)}, bf...) custom-call(s32[8]{0:T(128)} %compare_select_fusion.3.refs_0_.place_ref, ...), custom_call_target="tpu_custom_call" | custom-call | flops 4000000000 | bytes 2097152 | tf_op jit(solution)/shard_map/refine_own/pallas_call | solution.py:283
  19.8 0.0 all-to-all-done.refs_1_
  19.8 0.0 copy-start.1
  19.8 0.8 copy-done.1
  20.6 20.9 %refine_far.1 = bf16[16,104,128]{2,1,0:T(8,128)(2,1)} custom-call(s32[8]{0:T(128)} %compare_select_fusion.3.refs_0_.place_ref, bf16[4,16,4224]{2,1,0:T(8,128)(2,1)} %copy-done.1, bf16[16,104,128]{2,1,0:T(8,128)(2,1)} %get-tuple-element.27.refs_2_, bf16[144,128]{1,0:T(8,128)(2,1)} %bitcast.26, bf16[128,144]{1,0:T(8,128)(2,1)} %get-tuple-element.20.refs_4_, ...), custom_call_target="tpu_custom_call" | custom-call | flops 8000000000 | bytes 4194304 | tf_op jit(solution)/shard_map/refine_far/pallas_call | solution.py:283
  41.5 6.4 %all-to-all-start.2 = ((bf16[16,104,128]{2,1,0:T(8,128)(2,1)}), bf16[16,104,128]{2,1,0:T(8,128)(2,1)S(1)}, u32[]{:S(2)}, u32[]{:S(2)}) async-start(bf16[16,104,128]{2,1,0:T(8,128)(2,1)} %refine_far.1), calls=%async_computation.2 | async-start | bytes 851968 | tf_op jit(solution)/shard_map/all_to_all | solution.py:533
  47.9 11.7 %refine_near.1 = bf16[16,104,128]{2,1,0:T(8,128)(2,1)} custom-call(s32[8]{0:T(128)} %compare_select_fusion.3.refs_0_.place_ref, bf16[4,16,4224]{2,1,0:T(8,128)(2,1)} %copy-done.1, bf16[16,104,128]{2,1,0:T(8,128)(2,1)} %get-tuple-element.27.refs_2_, bf16[144,128]{1,0:T(8,128)(2,1)} %bitcast.27, ...), custom_call_target="tpu_custom_call", output_to_operand_aliasing={{}: (2, {})} | custom-call | flops 4000000000 | bytes 2097152 | tf_op jit(solution)/shard_map/refine_near/pallas_call | solution.py:283
  59.6 1.0 all-to-all-done.2
  60.6 5.0 %all-to-all-start.1 = ((bf16[16,104,128]{2,1,0:T(8,128)(2,1)}), bf16[16,104,128]{2,1,0:T(8,128)(2,1)S(1)}, u32[]{:S(2)}, u32[]{:S(2)}) async-start(bf16[16,104,128]{2,1,0:T(8,128)(2,1)} %refine_near.1), calls=%async_computation.1 | async-start | bytes 851968 | tf_op jit(solution)/shard_map/all_to_all | solution.py:536
  65.6 1.5 %collective-permute-start = (bf16[16,104,128]{2,1,0:T(8,128)(2,1)S(1)}, bf16[16,104,128]{2,1,0:T(8,128)(2,1)S(1)}, u32[]{:S(2)}, u32[]{:S(2)}) collective-permute-start(bf16[16,104,128]{2,1,0:T(8,128)(2,1)S(1)} %all-to-all-done.2), channel_id=1, source_target_pairs={{0,16},{16,0},{1,17},{17,1},{2,18},{18,2},{3,19},{19,3},{4,20},{20... | collective-permute-start | bytes 1277960 | tf_op jit(solution)/shard_map/ppermute | solution.py:537
  67.2 2.7 %flip.1 = (bf16[192,432]{1,0:T(8,128)(2,1)}, bf16[192,704]{1,0:T(8,128)(2,1)}, bf16[192,512]{1,0:T(8,128)(2,1)}, bf16[192,512]{1,0:T(8,128)(2,1)}, bf16[192,704]{1,0:T(8,128)(2,1)}) custom-call(bf16[432,192]{1,0:T(8,128)(2,1)} %bitcast.18, bf16[1728,192]{1,0:T(8,128)(2,1)} %bitcast.16), custom_call_target="tpu_custom_call" | custom-call | flops 1000000 | bytes 2097152 | tf_op jit(solution)/shard_map/flip/pallas_call | solution.py:472
  69.9 8.4 %all-to-all-done.1.near_ref = bf16[16,104,128]{2,1,0:T(8,128)(2,1)S(1)} async-done(((bf16[16,104,128]{2,1,0:T(8,128)(2,1)}), bf16[16,104,128]{2,1,0:T(8,128)(2,1)S(1)}, u32[]{:S(2)}, u32[]{:S(2)}) %all-to-all-start.1) | async-done | bytes 426016 | tf_op jit(solution)/shard_map/all_to_all | solution.py:536
  78.3 0.0 copy-start
  78.3 0.0 collective-permute-done.far_ref
  78.3 0.0 copy-start.2
  78.3 0.7 copy-done
  79.0 0.2 copy-done.2
  79.2 22.0 %decode.1 = bf16[4,192,8,512]{3,2,1,0:T(8,128)(2,1)} custom-call(s32[8]{0:T(128)} %compare_select_fusion.3.refs_0_.place_ref, bf16[16,104,128]{2,1,0:T(8,128)(2,1)} %copy-done, bf16[16,104,128]{2,1,0:T(8,128)(2,1)} %copy-done.2, bf16[192,432]{1,0:T(8,128)(2,1)} %get-tuple-element.28.t_in, bf16[192,704]{1,0:T(8,128)(2,1)} %get-tuple-element.29.t_a, ...), custom_call_target="tpu_custom_call" | custom-call | tf_op jit(solution)/shard_map/decode/pallas_call | solution.py:491
Async XLA Ops:
  1.9 17.9 %all-to-all-start = ((bf16[4,16,4224]{2,1,0:T(8,128)(2,1)}), bf16[4,16,4224]{2,1,0:T(8,128)(2,1)S(1)}, u32[]{:S(2)}, u32[]{:S(2)}) async-start(bf16[4,16,4224]{2,1,0:T(8,128)(2,1)} %pick.1.refs_1_), calls=%async_computation | async-start | bytes 1081344 | tf_op jit(solution)/shard_map/all_to_all | solution.py:521
  19.8 0.8 copy-start.1
  41.5 19.1 %all-to-all-start.2 = ((bf16[16,104,128]{2,1,0:T(8,128)(2,1)}), bf16[16,104,128]{2,1,0:T(8,128)(2,1)S(1)}, u32[]{:S(2)}, u32[]{:S(2)}) async-start(bf16[16,104,128]{2,1,0:T(8,128)(2,1)} %refine_far.1), calls=%async_computation.2 | async-start | bytes 851968 | tf_op jit(solution)/shard_map/all_to_all | solution.py:533
  60.6 17.7 %all-to-all-start.1 = ((bf16[16,104,128]{2,1,0:T(8,128)(2,1)}), bf16[16,104,128]{2,1,0:T(8,128)(2,1)S(1)}, u32[]{:S(2)}, u32[]{:S(2)}) async-start(bf16[16,104,128]{2,1,0:T(8,128)(2,1)} %refine_near.1), calls=%async_computation.1 | async-start | bytes 851968 | tf_op jit(solution)/shard_map/all_to_all | solution.py:536
  65.6 12.6 %collective-permute-start = (bf16[16,104,128]{2,1,0:T(8,128)(2,1)S(1)}, bf16[16,104,128]{2,1,0:T(8,128)(2,1)S(1)}, u32[]{:S(2)}, u32[]{:S(2)}) collective-permute-start(bf16[16,104,128]{2,1,0:T(8,128)(2,1)S(1)} %all-to-all-done.2), channel_id=1, source_target_pairs={{0,16},{16,0},{1,17},{17,1},{2,18},{18,2},{3,19},{19,3},{4,20},{20... | collective-permute-start | bytes 1277960 | tf_op jit(solution)/shard_map/ppermute | solution.py:537
  78.3 0.8 copy-start
  78.3 0.9 copy-start.2
